TPU v7x, 32 devices: a whole 2x2x4 slice. The times are simulated.
32 devices in a mesh: wide: 8 (over z, x), narrow: 4 (over y, core).
Axes of the slice: x: 2, y: 2, z: 4, core: 2. Of those that a mesh axis runs over, the one named last changes fastest.
Arguments:
- states: bfloat16 [256, 262144], P('narrow', 'wide'), may hold values from -6 to 6
- obs_ens: bfloat16 [256, 32768], P('narrow', 'wide'), may hold values from -6 to 6
- obs_value: float32 [32768], P('wide'), may hold values from -6 to 6
- obs_prec: float32 [32768], P('wide'), may hold values from 0.1 to 1
- obs_pick: int32 [32, 1024], P('wide'), may hold values from 0 to 4607, as said below
- taper: float32 [32, 1024], P(('wide', 'narrow')), may hold values from 0.1 to 1
Outputs:
- analysis: bfloat16 [256, 262144], P('narrow', 'wide')
Inputs may be any that keep to these rules, and one draw needn't show every extreme that they name: `obs_pick`: within a region the 1024 rows are distinct.
All inputs are finite; a program needn't handle non-finite values.
Results may differ from a plain program's by a relative error of at most 0.0057.
Values may be sent and summed in bfloat16 or wider, within the bound.
No kernel may reach another device: no remote copies, remote signals or barrier semaphores. Data moves between devices by JAX's collectives and lax.ppermute only.
A program may use at most 64 MiB of HBM per device.

v0:
```python
import functools

import jax
import jax.numpy as jnp
from jax import lax
from jax.experimental import pallas as pl
from jax.experimental.pallas import tpu as pltpu
from jax.sharding import PartitionSpec as P

HALO = 256
ITERS = 6
LANES = 128
FIRST = [(0, 2), (2, 3), (5, 3)]
OTHERS = [(0, 5), (5, 3)]
STEPS = [(0, 2), (2, 3), (5, 2), (7, 1)]


VMEM = pl.BlockSpec(memory_space=pltpu.VMEM)
SMEM = pl.BlockSpec(memory_space=pltpu.SMEM)
HBM = pl.BlockSpec(memory_space=pltpu.HBM)


def params():
    return pltpu.CompilerParams(vmem_limit_bytes=16 << 20)


def cost(flops, moved):
    return pl.CostEstimate(flops=flops, bytes_accessed=moved, transcendentals=0)


def swap(array, d):
    n = lax.axis_size("narrow")
    return lax.ppermute(array, "narrow", [(i, i ^ d) for i in range(n)])


def halo(last, first, flip):
    size, n = lax.axis_size("wide"), lax.axis_size("narrow")
    up = [(w * n + i, (w + 1) % size * n + (i ^ flip)) for w in range(size) for i in range(n)]
    down = [(w * n + i, (w - 1) % size * n + (i ^ flip)) for w in range(size) for i in range(n)]
    before = lax.ppermute(last, ("wide", "narrow"), up)
    after = lax.ppermute(first, ("wide", "narrow"), down)
    return before, after


def pack_kernel(partners, cells, start, states_ref, *refs):
    count = len(partners)
    outs, sems = refs[:count], refs[count]
    pos = lax.axis_index("narrow")
    width = outs[0].shape[1]
    copies = []
    for k, d in enumerate(partners):
        column = pl.multiple_of((pos ^ d) * cells + start, LANES)
        copies.append(
            pltpu.make_async_copy(states_ref.at[:, pl.ds(column, width)], outs[k], sems.at[k])
        )
        copies[-1].start()
    for copy in copies:
        copy.wait()


def pack(states, partners, cells, start, width):
    rows = states.shape[0]
    count = len(partners)
    return pl.pallas_call(
        functools.partial(pack_kernel, partners, cells, start),
        in_specs=[HBM],
        out_specs=[VMEM] * count,
        out_shape=[pltpu.VMEM((rows, width), jnp.bfloat16)] * count,
        scratch_shapes=[pltpu.SemaphoreType.DMA((count,))],
        compiler_params=params(),
        cost_estimate=cost(0, 4 * count * rows * width),
        name="pack",
    )(states)


def edges_kernel(*refs):
    outs = refs[-2:]
    rows = refs[0].shape[0]
    for k, out_ref in enumerate(outs):
        ens_ref, value_ref, prec_ref = refs[3 * k : 3 * k + 3]
        out_ref[:rows, :] = ens_ref[...].astype(jnp.float32)
        blank = jnp.zeros((6, out_ref.shape[1]), jnp.float32)
        out_ref[rows:, :] = jnp.concatenate([value_ref[...], prec_ref[...], blank], axis=0)


def edges(obs_ens, value, prec, width):
    rows, length = obs_ens.shape
    specs = [
        pl.BlockSpec((count, width), lambda i, at=at: (0, at))
        for at in (length // width - 1, 0)
        for count in (rows, 1, 1)
    ]
    shape = (rows + 8, width)
    return pl.pallas_call(
        edges_kernel,
        grid=(1,),
        in_specs=specs,
        out_specs=[pl.BlockSpec(shape, lambda i: (0, 0))] * 2,
        out_shape=[jax.ShapeDtypeStruct(shape, jnp.float32)] * 2,
        compiler_params=params(),
        cost_estimate=cost(0, 16 * rows * width),
        name="edges",
    )(*([obs_ens, value, prec] * 2))


def gather_kernel(regions, pick_ref, *refs):
    parts, outs, (table_ref, rows_ref) = refs[: -2 - regions], refs[-2 - regions : -2], refs[-2:]
    rows = table_ref.shape[1] // 2
    base = 0
    for own_ref, other_ref in zip(parts[::2], parts[1::2]):
        for k in range(own_ref.shape[1] // LANES):
            block = jnp.concatenate(
                [
                    r[:rows, k * LANES : (k + 1) * LANES].astype(jnp.float32)
                    for r in (own_ref, other_ref)
                ],
                axis=0,
            )
            table_ref[base : base + LANES, :] = block.T
            base += LANES
    step = 16
    used = rows_ref.shape[0]
    pos = lax.axis_index("narrow")

    for region in range(regions):

        def move(g, carry):
            for u in range(step):
                j = g * step + u
                row = pick_ref[pos ^ (2 * region), j]
                rows_ref[pl.ds(j, 1), :] = table_ref[pl.ds(row, 1), :]
            return carry

        lax.fori_loop(0, used // step, move, 0)
        outs[region][...] = rows_ref[...].astype(jnp.bfloat16)


def gather(picks, parts, rows):
    window = sum(p.shape[1] for p in parts[::2])
    regions, used = picks.shape[0] // 2, picks.shape[1]
    return pl.pallas_call(
        functools.partial(gather_kernel, regions),
        in_specs=[SMEM] + [VMEM] * len(parts),
        out_specs=[VMEM] * regions,
        out_shape=[jax.ShapeDtypeStruct((used, 2 * rows), jnp.bfloat16)] * regions,
        scratch_shapes=[
            pltpu.VMEM((window, 2 * rows), jnp.float32),
            pltpu.VMEM((used, 2 * rows), jnp.float32),
        ],
        compiler_params=params(),
        cost_estimate=cost(0, 16 * rows * (window + regions * used)),
        name="gather",
    )(picks, *parts)


def stats_kernel(pick_ref, taper_ref, before_ref, value_ref, prec_ref, after_ref, out_ref, table_ref):
    width = before_ref.shape[1]
    cuts = [slice(k, k + LANES) for k in range(0, width, LANES)]
    blocks = [before_ref[-8:, cut] for cut in cuts]
    blank = jnp.zeros((6, LANES), jnp.float32)
    for k in range(0, value_ref.shape[1], LANES):
        cut = slice(k, k + LANES)
        blocks.append(jnp.concatenate([value_ref[:, cut], prec_ref[:, cut], blank], axis=0))
    blocks += [after_ref[-8:, cut] for cut in cuts]
    for k, block in enumerate(blocks):
        table_ref[k * LANES : (k + 1) * LANES, :] = block.T
    step = 16
    used = out_ref.shape[0]
    pos = lax.axis_index("narrow")

    def move(g, carry):
        for u in range(step):
            j = g * step + u
            out_ref[pl.ds(j, 1), :] = table_ref[pl.ds(pick_ref[pos, j], 1), :]
        return carry

    lax.fori_loop(0, used // step, move, 0)
    for k in range(used // LANES):
        cut = slice(k * LANES, (k + 1) * LANES)
        column = jnp.broadcast_to(taper_ref[:, cut], (8, LANES)).T
        lane = lax.broadcasted_iota(jnp.int32, (LANES, 8), 1)
        out_ref[cut, :] = out_ref[cut, :] * jnp.where(lane == 1, column, 1.0)


def stats(picks, taper, parts):
    before, value, _, after = parts
    window = before.shape[1] + value.shape[1] + after.shape[1]
    used = picks.shape[1]
    return pl.pallas_call(
        stats_kernel,
        in_specs=[SMEM] + [VMEM] * (1 + len(parts)),
        out_specs=VMEM,
        out_shape=jax.ShapeDtypeStruct((used, 8), jnp.float32),
        scratch_shapes=[pltpu.VMEM((window, 8), jnp.float32)],
        compiler_params=params(),
        cost_estimate=cost(0, 512 * (window + used)),
        name="stats",
    )(picks, taper, *parts)


def dot(a, b):
    return jnp.dot(a, b, precision=lax.Precision.HIGHEST, preferred_element_type=jnp.float32)


def transform_kernel(own_ref, stats_ref, *refs):
    others, out_ref = refs[:-1], refs[-1]
    ensemble = jnp.concatenate([own_ref[...]] + [r[...] for r in others], axis=1).astype(jnp.float32)
    members = ensemble.shape[1]
    value, weight = stats_ref[:, 0:1], stats_ref[:, 1:2]
    mean = jnp.sum(ensemble, axis=1, keepdims=True) * (1.0 / members)
    pert = ensemble - mean
    scaled = (pert * jnp.sqrt(weight)).astype(jnp.bfloat16)
    forcing = jnp.sum(pert * (weight * (value - mean)), axis=0, keepdims=True)
    row = lax.broadcasted_iota(jnp.int32, (members, members), 0)
    column = lax.broadcasted_iota(jnp.int32, (members, members), 1)
    identity = jnp.where(row == column, 1.0, 0.0)
    matrix = (members - 1.0) * identity + lax.dot_general(
        scaled, scaled, (((0,), (0,)), ((), ())), preferred_element_type=jnp.float32
    )
    squares = jnp.sum(jnp.sum(matrix * matrix, axis=0, keepdims=True), axis=1, keepdims=True)
    norm_scale = jnp.sqrt(squares)
    current = matrix / norm_scale
    root = 1.5 * identity - 0.5 * current
    current = dot(current, root)
    for iteration in range(1, ITERS):
        middle = 1.5 * identity - 0.5 * dot(root, current)
        if iteration < ITERS - 1:
            current = dot(current, middle)
        root = dot(middle, root)
    inv_root = root / jnp.sqrt(norm_scale)
    forcing = jnp.broadcast_to(forcing, (8, members))
    mean_weights = dot(dot(forcing, inv_root), inv_root)[0:1]
    out_ref[...] = (jnp.sqrt(jnp.float32(members - 1)) * inv_root + mean_weights).astype(jnp.bfloat16)


def transform(picked, stat, others):
    used, pair = picked.shape
    members = pair * (1 + len(others))
    return pl.pallas_call(
        transform_kernel,
        grid=(1,),
        in_specs=[
            pl.BlockSpec((used, pair), lambda i: (0, 0)),
            pl.BlockSpec((used, 8), lambda i: (0, 0)),
        ]
        + [pl.BlockSpec((used, pair), lambda i: (0, 0))] * len(others),
        out_specs=pl.BlockSpec((members, members), lambda i: (0, 0)),
        out_shape=jax.ShapeDtypeStruct((members, members), jnp.bfloat16),
        compiler_params=params(),
        cost_estimate=cost(16 * 6 * 2 * members**3, 4 * used * members),
        name="transform",
    )(picked, stat, *others)


def apply_kernel(parts, at_ref, weights_ref, *refs):
    del at_ref
    sources, outs = refs[:parts], refs[-parts:]
    pieces = [r[...].astype(jnp.float32) for r in sources]
    rows = pieces[0].shape[0]
    total = sum(jnp.sum(p, axis=0, keepdims=True) for p in pieces)
    mean = total * (1.0 / (rows * parts))
    pert = jnp.concatenate([(p - mean).astype(jnp.bfloat16) for p in pieces], axis=0)
    mixed = jnp.dot(weights_ref[...], pert, preferred_element_type=jnp.float32)
    result = (mixed + mean).astype(jnp.bfloat16)
    for d in range(parts):
        outs[d][...] = result[d * rows : (d + 1) * rows]


def apply(weights, states, arrived, offsets, result, at, blocks, block):
    rows = states.shape[0]
    width = blocks * block
    parts = len(arrived) + 1
    members = rows * parts

    def far(offset):
        return pl.BlockSpec((rows, block), lambda i, at: (0, offset + i))

    near = pl.BlockSpec((rows, block), lambda i, at: (0, at[0] + i))
    given = [] if result is None else [result]
    return pl.pallas_call(
        functools.partial(apply_kernel, parts),
        grid_spec=pltpu.PrefetchScalarGridSpec(
            num_scalar_prefetch=1,
            grid=(blocks,),
            in_specs=[pl.BlockSpec((members, members), lambda i, at: (0, 0)), near]
            + [far(offset) for offset in offsets]
            + [HBM] * len(given),
            out_specs=[near] + [far(0)] * (parts - 1),
        ),
        out_shape=[jax.ShapeDtypeStruct(states.shape, jnp.bfloat16)]
        + [jax.ShapeDtypeStruct((rows, width), jnp.bfloat16)] * (parts - 1),
        input_output_aliases={2 + parts: 0} if given else {},
        compiler_params=params(),
        cost_estimate=cost(2 * members * members * width, 4 * members * width),
        name="apply",
    )(at, weights, states, *arrived, *given)


def place_kernel(cells, start, partners, result_ref, *refs):
    del result_ref
    parts, out_ref, sems = refs[:-2], refs[-2], refs[-1]
    pos = lax.axis_index("narrow")
    copies = []
    for k, part in enumerate(parts):
        column = pl.multiple_of((pos ^ partners[k]) * cells + start, LANES)
        copies.append(
            pltpu.make_async_copy(part, out_ref.at[:, pl.ds(column, part.shape[1])], sems.at[k])
        )
        copies[-1].start()
    for copy in copies:
        copy.wait()


def place(result, parts, cells, start, partners):
    return pl.pallas_call(
        functools.partial(place_kernel, cells, start, partners),
        in_specs=[HBM] + [VMEM] * len(parts),
        out_specs=HBM,
        out_shape=jax.ShapeDtypeStruct(result.shape, result.dtype),
        scratch_shapes=[pltpu.SemaphoreType.DMA((len(parts),))],
        input_output_aliases={0: 0},
        compiler_params=params(),
        cost_estimate=cost(0, sum(4 * p.size for p in parts)),
        name="place",
    )(result, *parts)


def body(states, obs_ens, obs_value, obs_prec, obs_pick, taper):
    n = lax.axis_size("narrow")
    pos = lax.axis_index("narrow")
    cells = states.shape[1] // n
    unit = cells // 8
    states = pltpu.with_memory_space_constraint(states, pltpu.HBM)

    arrived = {d: [] for d in range(1, n)}

    def send(partners, first, count):
        parts = pack(states, partners, cells, first * unit, count * unit)
        for d, part in zip(partners, parts):
            arrived[d].append((first, count, swap(part, d)))

    far = list(range(2, n))
    send(far[:1], *FIRST[0])
    send(far[1:], *OTHERS[0])
    send(far[:1], *FIRST[1])
    send(far, *OTHERS[1])
    send([1], 0, 8)

    other = swap(obs_ens, 1)
    value, prec = obs_value.reshape(1, -1), obs_prec.reshape(1, -1)
    last, first = edges(obs_ens, value, prec, HALO)
    before, after = halo(last, first, 0)
    other_before, other_after = halo(last, first, 1)
    rows = states.shape[0]
    picked = gather(obs_pick, [before, other_before, obs_ens, other, after, other_after], rows)
    others = []
    for d in far[::2]:
        others.append(swap(picked[d // 2], d))
    stat = stats(obs_pick, taper, [before, value, prec, after])
    weights = transform(picked[0], stat, others)

    result, outgoing = None, []
    for first, count in STEPS:
        at = jnp.reshape((pos * cells) // unit + first, (1,))
        parts, offsets = [], []
        for d in range(1, n):
            for base, units, part in arrived[d]:
                if base <= first < base + units:
                    parts.append(part)
                    offsets.append(first - base)
        result, *leaving = apply(weights, states, parts, offsets, result, at, count, unit)
        moved = []
        for d, part in enumerate(leaving, 1):
            moved.append(swap(part, d))
        outgoing.append((first, moved))
    for first, moved in outgoing:
        cut = n - 1 if first != STEPS[-1][0] else n - 2
        partners = list(range(1, n))
        result = place(result, moved[:cut], cells, first * unit, partners[:cut])
        if cut < n - 1:
            result = place(result, moved[cut:], cells, first * unit, partners[cut:])
    return result


def solution(mesh):
    return jax.shard_map(
        body,
        mesh=mesh,
        in_specs=(
            P("narrow", "wide"),
            P("narrow", "wide"),
            P("wide"),
            P("wide"),
            P("wide", None),
            P(("wide", "narrow"), None),
        ),
        out_specs=P("narrow", "wide"),
        check_vma=False,
    )
```

profile of v0, /device:TPU:0, one launch (start us, length us, event | category | flops | bytes accessed | tf_op | source)
XLA Modules:
  0.0 107.1 jit_solution(12072378336618643808)
XLA Ops:
  0.0 0.6 collective-permute-start.2
  0.6 2.2 %pack.5 = bf16[64,8192]{1,0:T(8,128)(2,1)} custom-call(bf16[64,32768]{1,0:T(8,128)(2,1)} %refs_0_.9), custom_call_target="tpu_custom_call" | custom-call | bytes 2097152 | tf_op jit(solution)/shard_map/pack/pallas_call | solution.py:64
  2.8 0.1 collective-permute-start.6
  2.9 0.0 copy-start.11
  3.0 2.6 %collective-permute-start.1 = (f32[72,256]{1,0:T(8,128)S(1)}, f32[72,256]{1,0:T(8,128)S(1)}, u32[]{:S(2)}, u32[]{:S(2)}) collective-permute-start(f32[72,256]{1,0:T(8,128)S(1)} %get-tuple-element.27), channel_id=1, source_target_pairs={{0,5},{1,4},{2,7},{3,6},{4,9},{5,8},{6,11},{7,10},{8,13},{9,12},{1... | collective-permute-start | bytes 221192 | tf_op jit(solution)/shard_map/ppermute | solution.py:40
  5.6 1.5 %collective-permute-start = (f32[72,256]{1,0:T(8,128)S(1)}, f32[72,256]{1,0:T(8,128)S(1)}, u32[]{:S(2)}, u32[]{:S(2)}) collective-permute-start(f32[72,256]{1,0:T(8,128)S(1)} %get-tuple-element.27), channel_id=1, source_target_pairs={{0,4},{1,5},{2,6},{3,7},{4,8},{5,9},{6,10},{7,11},{8,12},{9,13},{1... | collective-permute-start | bytes 221192 | tf_op jit(solution)/shard_map/ppermute | solution.py:40
  7.1 1.1 %pack.8 = bf16[64,5120]{1,0:T(8,128)(2,1)S(1)} custom-call(bf16[64,32768]{1,0:T(8,128)(2,1)} %refs_0_.9), custom_call_target="tpu_custom_call" | custom-call | bytes 1310720 | tf_op jit(solution)/shard_map/pack/pallas_call | solution.py:64
  8.2 1.3 %collective-permute-start.10 = (bf16[64,5120]{1,0:T(8,128)(2,1)S(1)}, bf16[64,5120]{1,0:T(8,128)(2,1)S(1)}, u32[]{:S(2)}, u32[]{:S(2)}) collective-permute-start(bf16[64,5120]{1,0:T(8,128)(2,1)S(1)} %pack.8), channel_id=1, source_target_pairs={{0,3},{1,2},{2,1},{3,0},{4,7},{5,6},{6,5},{7,4},{8,11},{9,10},{10,... | collective-permute-start | bytes 1966088 | tf_op jit(solution)/shard_map/ppermute | solution.py:33
  9.6 1.2 %collective-permute-done.1.refs_1_ = f32[72,256]{1,0:T(8,128)S(1)} collective-permute-done((f32[72,256]{1,0:T(8,128)S(1)}, f32[72,256]{1,0:T(8,128)S(1)}, u32[]{:S(2)}, u32[]{:S(2)}) %collective-permute-start.1) | collective-permute-done | bytes 73760 | tf_op jit(solution)/shard_map/ppermute | solution.py:40
  10.8 2.4 %collective-permute-start.4 = (f32[72,256]{1,0:T(8,128)S(1)}, f32[72,256]{1,0:T(8,128)S(1)}, u32[]{:S(2)}, u32[]{:S(2)}) collective-permute-start(f32[72,256]{1,0:T(8,128)S(1)} %get-tuple-element.28), channel_id=1, source_target_pairs={{0,29},{1,28},{2,31},{3,30},{4,1},{5,0},{6,3},{7,2},{8,5},{9,4},{1... | collective-permute-start | bytes 221192 | tf_op jit(solution)/shard_map/ppermute | solution.py:41
  13.2 0.0 collective-permute-done.refs_0_.before_ref
  13.2 1.9 %collective-permute-start.3 = (f32[72,256]{1,0:T(8,128)S(1)}, f32[72,256]{1,0:T(8,128)S(1)}, u32[]{:S(2)}, u32[]{:S(2)}) collective-permute-start(f32[72,256]{1,0:T(8,128)S(1)} %get-tuple-element.28), channel_id=1, source_target_pairs={{0,28},{1,29},{2,30},{3,31},{4,0},{5,1},{6,2},{7,3},{8,4},{9,5},{1... | collective-permute-start | bytes 221192 | tf_op jit(solution)/shard_map/ppermute | solution.py:41
  15.1 1.6 %pack.9 = bf16[64,2048]{1,0:T(8,128)(2,1)} custom-call(bf16[64,32768]{1,0:T(8,128)(2,1)} %refs_0_.9), custom_call_target="tpu_custom_call" | custom-call | bytes 524288 | tf_op jit(solution)/shard_map/pack/pallas_call | solution.py:64
  16.8 0.0 collective-permute-done.4.refs_5_
  16.8 1.6 %collective-permute-start.11 = (bf16[64,2048]{1,0:T(8,128)(2,1)}, bf16[64,2048]{1,0:T(8,128)(2,1)S(1)}, u32[]{:S(2)}, u32[]{:S(2)}) collective-permute-start(bf16[64,2048]{1,0:T(8,128)(2,1)} %pack.9), channel_id=1, source_target_pairs={{0,2},{1,3},{2,0},{3,1},{4,6},{5,7},{6,4},{7,5},{8,10},{9,11},{10,... | collective-permute-start | bytes 786440 | tf_op jit(solution)/shard_map/ppermute | solution.py:33
  18.4 7.6 %gather.1 = (bf16[1024,128]{1,0:T(8,128)(2,1)S(1)}, bf16[1024,128]{1,0:T(8,128)(2,1)}) custom-call(s32[4,1024]{1,0:T(4,128)S(1)} %copy-done.11, f32[72,256]{1,0:T(8,128)S(1)} %collective-permute-done.refs_0_.before_ref, f32[72,256]{1,0:T(8,128)S(1)} %collective-permute-done.1.refs_1_, bf16[64,4096]{1,0:T(8,128)(2,1)S(1)} %copy-done, ...), custom_call_target="tpu_custom_call" | custom-call | bytes 6815744 | tf_op jit(solution)/shard_map/gather/pallas_call | solution.py:141
  26.0 0.7 copy-done.15
  26.7 0.8 collective-permute-start.5
  27.5 1.7 %pack.7 = bf16[64,3072]{1,0:T(8,128)(2,1)} custom-call(bf16[64,32768]{1,0:T(8,128)(2,1)} %refs_0_.9), custom_call_target="tpu_custom_call" | custom-call | bytes 786432 | tf_op jit(solution)/shard_map/pack/pallas_call | solution.py:64
  29.3 1.3 %collective-permute-start.9 = (bf16[64,3072]{1,0:T(8,128)(2,1)}, bf16[64,3072]{1,0:T(8,128)(2,1)}, u32[]{:S(2)}, u32[]{:S(2)}) collective-permute-start(bf16[64,3072]{1,0:T(8,128)(2,1)} %pack.7), channel_id=1, source_target_pairs={{0,2},{1,3},{2,0},{3,1},{4,6},{5,7},{6,4},{7,5},{8,10},{9,11},{10,... | collective-permute-start | bytes 1179656 | tf_op jit(solution)/shard_map/ppermute | solution.py:33
  30.6 1.1 %pack.6 = (bf16[64,3072]{1,0:T(8,128)(2,1)S(1)}, bf16[64,3072]{1,0:T(8,128)(2,1)S(1)}) custom-call(bf16[64,32768]{1,0:T(8,128)(2,1)} %refs_0_.9), custom_call_target="tpu_custom_call" | custom-call | bytes 1572864 | tf_op jit(solution)/shard_map/pack/pallas_call | solution.py:64
  31.7 0.8 copy-done.14
  32.5 4.5 %stats.1.stats_ref = f32[1024,8]{1,0:T(8,128)S(1)} custom-call(s32[4,1024]{1,0:T(4,128)S(1)} %copy-done.11, f32[1,1024]{1,0:T(1,128)S(1)} %copy-done.12, f32[72,256]{1,0:T(8,128)S(1)} %collective-permute-done.refs_0_.before_ref, f32[1,4096]{1,0:T(1,128)S(1)} %bitcast.8, f32[1,4096]{1,0:T(1,128)S(1)} %bitcast.11, ...), custom_call_target="tpu_custom_call" | custom-call | bytes 2883584 | tf_op jit(solution)/shard_map/stats/pallas_call | solution.py:189
  37.0 0.0 collective-permute-done.11.refs_2_
  37.0 0.8 collective-permute-start.7
  37.8 0.9 copy-done.16
  38.8 8.5 %transform.1.weights_ref = bf16[256,256]{1,0:T(8,128)(2,1)S(1)} custom-call(bf16[1024,128]{1,0:T(8,128)(2,1)S(1)} %copy-done.16, f32[1024,8]{1,0:T(8,128)S(1)} %stats.1.stats_ref, bf16[1024,128]{1,0:T(8,128)(2,1)} %collective-permute-done.5.refs_0_), custom_call_target="tpu_custom_call" | custom-call | flops 3221225472 | bytes 1048576 | tf_op jit(solution)/shard_map/transform/pallas_call | solution.py:239
  47.3 0.0 collective-permute-done.10.refs_3_
  47.3 0.0 collective-permute-done.6.refs_1_
  47.4 2.5 %apply.4 = (bf16[64,32768]{1,0:T(8,128)(2,1)}, bf16[64,2048]{1,0:T(8,128)(2,1)}, bf16[64,2048]{1,0:T(8,128)(2,1)}, bf16[64,2048]{1,0:T(8,128)(2,1)S(1)}) custom-call(s32[1]{0:T(128)} %bitcast.5.at_ref, bf16[256,256]{1,0:T(8,128)(2,1)S(1)} %transform.1.weights_ref, bf16[64,32768]{1,0:T(8,128)(2,1)} %refs_0_.9, ...), custom_call_target="tpu_custom_call" | custom-call | flops 268435456 | bytes 2097152 | tf_op jit(solution)/shard_map/apply/pallas_call | solution.py:280
  49.9 0.7 copy-done.17
  50.6 1.4 %collective-permute-start.12 = (bf16[64,2048]{1,0:T(8,128)(2,1)}, bf16[64,2048]{1,0:T(8,128)(2,1)S(1)}, u32[]{:S(2)}, u32[]{:S(2)}) collective-permute-start(bf16[64,2048]{1,0:T(8,128)(2,1)} %get-tuple-element.37), channel_id=1, source_target_pairs={{0,1},{1,0},{2,3},{3,2},{4,5},{5,4},{6,7},{7,6},{8,9},{9,8},{10,11... | collective-permute-start | bytes 786440 | tf_op jit(solution)/shard_map/ppermute | solution.py:33
  52.0 0.8 collective-permute-start.13
  52.7 0.6 collective-permute-start.14
  53.3 3.7 %apply.5 = (bf16[64,32768]{1,0:T(8,128)(2,1)}, bf16[64,3072]{1,0:T(8,128)(2,1)}, bf16[64,3072]{1,0:T(8,128)(2,1)}, bf16[64,3072]{1,0:T(8,128)(2,1)}) custom-call(s32[1]{0:T(128)} %bitcast.4.at_ref, bf16[256,256]{1,0:T(8,128)(2,1)S(1)} %transform.1.weights_ref, bf16[64,32768]{1,0:T(8,128)(2,1)} %refs_0_.9, ...), custom_call_target="tpu_custom_call", output_to_operand_aliasing={{0}: (6, {})} | custom-call | flops 402653184 | bytes 3145728 | tf_op jit(solution)/shard_map/apply/pallas_call | solution.py:280
  57.0 0.8 collective-permute-start.15
  57.9 3.6 %collective-permute-done.8.refs_3_ = bf16[64,3072]{1,0:T(8,128)(2,1)S(1)} collective-permute-done((bf16[64,3072]{1,0:T(8,128)(2,1)}, bf16[64,3072]{1,0:T(8,128)(2,1)S(1)}, u32[]{:S(2)}, u32[]{:S(2)}) %collective-permute-start.8) | collective-permute-done | bytes 393248 | tf_op jit(solution)/shard_map/ppermute | solution.py:33
  61.5 2.5 %apply.6 = (bf16[64,32768]{1,0:T(8,128)(2,1)}, bf16[64,2048]{1,0:T(8,128)(2,1)S(1)}, bf16[64,2048]{1,0:T(8,128)(2,1)}, bf16[64,2048]{1,0:T(8,128)(2,1)}) custom-call(s32[1]{0:T(128)} %bitcast.3.at_ref, bf16[256,256]{1,0:T(8,128)(2,1)S(1)} %transform.1.weights_ref, bf16[64,32768]{1,0:T(8,128)(2,1)} %refs_0_.9, ...), custom_call_target="tpu_custom_call", output_to_operand_aliasing={{0}: (6, {})} | custom-call | flops 268435456 | bytes 2097152 | tf_op jit(solution)/shard_map/apply/pallas_call | solution.py:280
  64.1 0.5 collective-permute-start.18
  64.6 0.7 copy-done.1
  65.3 1.5 %collective-permute-start.16 = (bf16[64,3072]{1,0:T(8,128)(2,1)}, bf16[64,3072]{1,0:T(8,128)(2,1)S(1)}, u32[]{:S(2)}, u32[]{:S(2)}) collective-permute-start(bf16[64,3072]{1,0:T(8,128)(2,1)} %get-tuple-element.41), channel_id=1, source_target_pairs={{0,2},{1,3},{2,0},{3,1},{4,6},{5,7},{6,4},{7,5},{8,10},{9,11},{10,... | collective-permute-start | bytes 1179656 | tf_op jit(solution)/shard_map/ppermute | solution.py:33
  66.8 1.0 collective-permute-done.13.refs_1_
  67.8 0.7 copy-done.3
  68.5 0.6 collective-permute-start.17
  69.1 3.7 %collective-permute-done.14.refs_2_ = bf16[64,2048]{1,0:T(8,128)(2,1)S(1)} collective-permute-done((bf16[64,2048]{1,0:T(8,128)(2,1)}, bf16[64,2048]{1,0:T(8,128)(2,1)S(1)}, u32[]{:S(2)}, u32[]{:S(2)}) %collective-permute-start.14) | collective-permute-done | bytes 262176 | tf_op jit(solution)/shard_map/ppermute | solution.py:33
  72.8 0.7 copy-done.5
  73.5 1.5 %collective-permute-start.19 = (bf16[64,2048]{1,0:T(8,128)(2,1)}, bf16[64,2048]{1,0:T(8,128)(2,1)}, u32[]{:S(2)}, u32[]{:S(2)}) collective-permute-start(bf16[64,2048]{1,0:T(8,128)(2,1)} %get-tuple-element.44), channel_id=1, source_target_pairs={{0,2},{1,3},{2,0},{3,1},{4,6},{5,7},{6,4},{7,5},{8,10},{9,11},{10,... | collective-permute-start | bytes 786440 | tf_op jit(solution)/shard_map/ppermute | solution.py:33
  75.0 0.7 copy-done.7
  75.7 0.3 collective-permute-start.20
  76.0 2.0 %apply.7 = (bf16[64,32768]{1,0:T(8,128)(2,1)}, bf16[64,1024]{1,0:T(8,128)(2,1)S(1)}, bf16[64,1024]{1,0:T(8,128)(2,1)S(1)}, bf16[64,1024]{1,0:T(8,128)(2,1)S(1)}) custom-call(s32[1]{0:T(128)} %bitcast.at_ref, bf16[256,256]{1,0:T(8,128)(2,1)S(1)} %transform.1.weights_ref, bf16[64,32768]{1,0:T(8,128)(2,1)} %refs_0_.9, ...), custom_call_target="tpu_custom_call", output_to_operand_aliasing={{0}: (6, {})} | custom-call | flops 134217728 | bytes 1048576 | tf_op jit(solution)/shard_map/apply/pallas_call | solution.py:280
  78.0 0.3 collective-permute-start.21
  78.3 3.6 %collective-permute-done.16.refs_1_ = bf16[64,3072]{1,0:T(8,128)(2,1)S(1)} collective-permute-done((bf16[64,3072]{1,0:T(8,128)(2,1)}, bf16[64,3072]{1,0:T(8,128)(2,1)S(1)}, u32[]{:S(2)}, u32[]{:S(2)}) %collective-permute-start.16) | collective-permute-done | bytes 393248 | tf_op jit(solution)/shard_map/ppermute | solution.py:33
  81.9 1.5 %collective-permute-start.22 = (bf16[64,1024]{1,0:T(8,128)(2,1)S(1)}, bf16[64,1024]{1,0:T(8,128)(2,1)S(1)}, u32[]{:S(2)}, u32[]{:S(2)}) collective-permute-start(bf16[64,1024]{1,0:T(8,128)(2,1)S(1)} %get-tuple-element.47), channel_id=1, source_target_pairs={{0,2},{1,3},{2,0},{3,1},{4,6},{5,7},{6,4},{7,5},{8,10},{9,11},{10,... | collective-permute-start | bytes 393224 | tf_op jit(solution)/shard_map/ppermute | solution.py:33
  83.4 6.2 %collective-permute-done.17.refs_2_ = bf16[64,3072]{1,0:T(8,128)(2,1)S(1)} collective-permute-done((bf16[64,3072]{1,0:T(8,128)(2,1)}, bf16[64,3072]{1,0:T(8,128)(2,1)S(1)}, u32[]{:S(2)}, u32[]{:S(2)}) %collective-permute-start.17) | collective-permute-done | bytes 393248 | tf_op jit(solution)/shard_map/ppermute | solution.py:33
  89.6 1.6 %collective-permute-start.23 = (bf16[64,1024]{1,0:T(8,128)(2,1)S(1)}, bf16[64,1024]{1,0:T(8,128)(2,1)S(1)}, u32[]{:S(2)}, u32[]{:S(2)}) collective-permute-start(bf16[64,1024]{1,0:T(8,128)(2,1)S(1)} %get-tuple-element.48), channel_id=1, source_target_pairs={{0,3},{1,2},{2,1},{3,0},{4,7},{5,6},{6,5},{7,4},{8,11},{9,10},{10,... | collective-permute-start | bytes 393224 | tf_op jit(solution)/shard_map/ppermute | solution.py:33
  91.2 0.9 place.5.result_ref
  92.2 1.0 place.6.result_ref
  93.2 2.8 %collective-permute-done.19.refs_1_ = bf16[64,2048]{1,0:T(8,128)(2,1)} collective-permute-done((bf16[64,2048]{1,0:T(8,128)(2,1)}, bf16[64,2048]{1,0:T(8,128)(2,1)}, u32[]{:S(2)}, u32[]{:S(2)}) %collective-permute-start.19) | collective-permute-done | bytes 262176 | tf_op jit(solution)/shard_map/ppermute | solution.py:33
  96.0 4.9 %collective-permute-done.20.refs_2_ = bf16[64,2048]{1,0:T(8,128)(2,1)} collective-permute-done((bf16[64,2048]{1,0:T(8,128)(2,1)}, bf16[64,2048]{1,0:T(8,128)(2,1)}, u32[]{:S(2)}, u32[]{:S(2)}) %collective-permute-start.20) | collective-permute-done | bytes 262176 | tf_op jit(solution)/shard_map/ppermute | solution.py:33
  100.9 1.9 %place.7.result_ref = bf16[64,32768]{1,0:T(8,128)(2,1)} custom-call(bf16[64,32768]{1,0:T(8,128)(2,1)} %place.6.result_ref, bf16[64,2048]{1,0:T(8,128)(2,1)S(1)} %copy-done.8, bf16[64,2048]{1,0:T(8,128)(2,1)} %collective-permute-done.19.refs_1_, bf16[64,2048]{1,0:T(8,128)(2,1)} %collective-permute-done.20.refs_2_), custom_call_target="tpu_custom_call", output_to_operand_aliasing={{}: (0, {})} | custom-call | bytes 1572864 | tf_op jit(solution)/shard_map/place/pallas_call | solution.py:315
  102.9 1.4 %collective-permute-done.22.refs_1_ = bf16[64,1024]{1,0:T(8,128)(2,1)S(1)} collective-permute-done((bf16[64,1024]{1,0:T(8,128)(2,1)S(1)}, bf16[64,1024]{1,0:T(8,128)(2,1)S(1)}, u32[]{:S(2)}, u32[]{:S(2)}) %collective-permute-start.22) | collective-permute-done | bytes 131104 | tf_op jit(solution)/shard_map/ppermute | solution.py:33
  104.3 0.7 place.8.result_ref
  105.0 1.4 %collective-permute-done.23.refs_0_ = bf16[64,1024]{1,0:T(8,128)(2,1)S(1)} collective-permute-done((bf16[64,1024]{1,0:T(8,128)(2,1)S(1)}, bf16[64,1024]{1,0:T(8,128)(2,1)S(1)}, u32[]{:S(2)}, u32[]{:S(2)}) %collective-permute-start.23) | collective-permute-done | bytes 131104 | tf_op jit(solution)/shard_map/ppermute | solution.py:33
  106.5 0.7 place.9
  (38 shorter events, 0.1 us)
Async XLA Ops:
  0.0 2.9 %copy-start = (bf16[64,4096]{1,0:T(8,128)(2,1)S(1)}, bf16[64,4096]{1,0:T(8,128)(2,1)}, u32[]{:S(2)}) copy-start(bf16[64,4096]{1,0:T(8,128)(2,1)} %refs_2_.1) | copy-start | bytes 1572868
  0.0 2.9 %copy-start.10 = (f32[4096]{0:T(1024)S(1)}, f32[4096]{0:T(1024)}, u32[]{:S(2)}) copy-start(f32[4096]{0:T(1024)} %param.9) | copy-start | bytes 49156
  0.0 2.9 %copy-start.9 = (f32[4096]{0:T(1024)S(1)}, f32[4096]{0:T(1024)}, u32[]{:S(2)}) copy-start(f32[4096]{0:T(1024)} %param.8) | copy-start | bytes 49156
  0.0 18.4 %collective-permute-start.2 = (bf16[64,4096]{1,0:T(8,128)(2,1)}, bf16[64,4096]{1,0:T(8,128)(2,1)S(1)}, u32[]{:S(2)}, u32[]{:S(2)}) collective-permute-start(bf16[64,4096]{1,0:T(8,128)(2,1)} %refs_2_.1), channel_id=1, source_target_pairs={{0,1},{1,0},{2,3},{3,2},{4,5},{5,4},{6,7},{7,6},{8,9},{9,8},{10,11... | collective-permute-start | bytes 1572872 | tf_op jit(solution)/shard_map/ppermute | solution.py:33
  2.8 44.6 %collective-permute-start.6 = (bf16[64,8192]{1,0:T(8,128)(2,1)}, bf16[64,8192]{1,0:T(8,128)(2,1)S(1)}, u32[]{:S(2)}, u32[]{:S(2)}) collective-permute-start(bf16[64,8192]{1,0:T(8,128)(2,1)} %pack.5), channel_id=1, source_target_pairs={{0,1},{1,0},{2,3},{3,2},{4,5},{5,4},{6,7},{7,6},{8,9},{9,8},{10,11... | collective-permute-start | bytes 3145736 | tf_op jit(solution)/shard_map/ppermute | solution.py:33
  2.9 15.4 %copy-start.11 = (s32[4,1024]{1,0:T(4,128)S(1)}, s32[4,1024]{1,0:T(4,128)}, u32[]{:S(2)}) copy-start(s32[4,1024]{1,0:T(4,128)} %pick_ref.3) | copy-start | bytes 49156
  3.0 7.9 %collective-permute-start.1 = (f32[72,256]{1,0:T(8,128)S(1)}, f32[72,256]{1,0:T(8,128)S(1)}, u32[]{:S(2)}, u32[]{:S(2)}) collective-permute-start(f32[72,256]{1,0:T(8,128)S(1)} %get-tuple-element.27), channel_id=1, source_target_pairs={{0,5},{1,4},{2,7},{3,6},{4,9},{5,8},{6,11},{7,10},{8,13},{9,12},{1... | collective-permute-start | bytes 221192 | tf_op jit(solution)/shard_map/ppermute | solution.py:40
  5.6 7.6 %collective-permute-start = (f32[72,256]{1,0:T(8,128)S(1)}, f32[72,256]{1,0:T(8,128)S(1)}, u32[]{:S(2)}, u32[]{:S(2)}) collective-permute-start(f32[72,256]{1,0:T(8,128)S(1)} %get-tuple-element.27), channel_id=1, source_target_pairs={{0,4},{1,5},{2,6},{3,7},{4,8},{5,9},{6,10},{7,11},{8,12},{9,13},{1... | collective-permute-start | bytes 221192 | tf_op jit(solution)/shard_map/ppermute | solution.py:40
  8.2 39.1 %collective-permute-start.10 = (bf16[64,5120]{1,0:T(8,128)(2,1)S(1)}, bf16[64,5120]{1,0:T(8,128)(2,1)S(1)}, u32[]{:S(2)}, u32[]{:S(2)}) collective-permute-start(bf16[64,5120]{1,0:T(8,128)(2,1)S(1)} %pack.8), channel_id=1, source_target_pairs={{0,3},{1,2},{2,1},{3,0},{4,7},{5,6},{6,5},{7,4},{8,11},{9,10},{10,... | collective-permute-start | bytes 1966088 | tf_op jit(solution)/shard_map/ppermute | solution.py:33
  10.8 5.9 %collective-permute-start.4 = (f32[72,256]{1,0:T(8,128)S(1)}, f32[72,256]{1,0:T(8,128)S(1)}, u32[]{:S(2)}, u32[]{:S(2)}) collective-permute-start(f32[72,256]{1,0:T(8,128)S(1)} %get-tuple-element.28), channel_id=1, source_target_pairs={{0,29},{1,28},{2,31},{3,30},{4,1},{5,0},{6,3},{7,2},{8,5},{9,4},{1... | collective-permute-start | bytes 221192 | tf_op jit(solution)/shard_map/ppermute | solution.py:41
  13.2 5.2 %collective-permute-start.3 = (f32[72,256]{1,0:T(8,128)S(1)}, f32[72,256]{1,0:T(8,128)S(1)}, u32[]{:S(2)}, u32[]{:S(2)}) collective-permute-start(f32[72,256]{1,0:T(8,128)S(1)} %get-tuple-element.28), channel_id=1, source_target_pairs={{0,28},{1,29},{2,30},{3,31},{4,0},{5,1},{6,2},{7,3},{8,4},{9,5},{1... | collective-permute-start | bytes 221192 | tf_op jit(solution)/shard_map/ppermute | solution.py:41
  16.8 20.2 %collective-permute-start.11 = (bf16[64,2048]{1,0:T(8,128)(2,1)}, bf16[64,2048]{1,0:T(8,128)(2,1)S(1)}, u32[]{:S(2)}, u32[]{:S(2)}) collective-permute-start(bf16[64,2048]{1,0:T(8,128)(2,1)} %pack.9), channel_id=1, source_target_pairs={{0,2},{1,3},{2,0},{3,1},{4,6},{5,7},{6,4},{7,5},{8,10},{9,11},{10,... | collective-permute-start | bytes 786440 | tf_op jit(solution)/shard_map/ppermute | solution.py:33
  26.0 0.7 copy-start.15
  26.7 5.8 %copy-start.12 = (f32[1,1024]{1,0:T(1,128)S(1)}, f32[1,1024]{1,0:T(1,128)}, u32[]{:S(2)}) copy-start(f32[1,1024]{1,0:T(1,128)} %taper_ref.1) | copy-start | bytes 12292
  26.7 11.1 %collective-permute-start.5 = (bf16[1024,128]{1,0:T(8,128)(2,1)}, bf16[1024,128]{1,0:T(8,128)(2,1)}, u32[]{:S(2)}, u32[]{:S(2)}) collective-permute-start(bf16[1024,128]{1,0:T(8,128)(2,1)} %get-tuple-element.30), channel_id=1, source_target_pairs={{0,2},{1,3},{2,0},{3,1},{4,6},{5,7},{6,4},{7,5},{8,10},{9,11},{10,... | collective-permute-start | bytes 786440 | tf_op jit(solution)/shard_map/ppermute | solution.py:33
  29.3 23.5 %collective-permute-start.9 = (bf16[64,3072]{1,0:T(8,128)(2,1)}, bf16[64,3072]{1,0:T(8,128)(2,1)}, u32[]{:S(2)}, u32[]{:S(2)}) collective-permute-start(bf16[64,3072]{1,0:T(8,128)(2,1)} %pack.7), channel_id=1, source_target_pairs={{0,2},{1,3},{2,0},{3,1},{4,6},{5,7},{6,4},{7,5},{8,10},{9,11},{10,... | collective-permute-start | bytes 1179656 | tf_op jit(solution)/shard_map/ppermute | solution.py:33
  31.7 0.8 copy-start.14
  32.5 4.5 %copy-start.13 = (bf16[64,3072]{1,0:T(8,128)(2,1)}, bf16[64,3072]{1,0:T(8,128)(2,1)S(1)}, u32[]{:S(2)}) copy-start(bf16[64,3072]{1,0:T(8,128)(2,1)S(1)} %get-tuple-element.32) | copy-start | bytes 1179652
  37.0 20.1 %collective-permute-start.7 = (bf16[64,3072]{1,0:T(8,128)(2,1)}, bf16[64,3072]{1,0:T(8,128)(2,1)S(1)}, u32[]{:S(2)}, u32[]{:S(2)}) collective-permute-start(bf16[64,3072]{1,0:T(8,128)(2,1)} %copy-done.14), channel_id=1, source_target_pairs={{0,2},{1,3},{2,0},{3,1},{4,6},{5,7},{6,4},{7,5},{8,10},{9,11},{10,... | collective-permute-start | bytes 1179656 | tf_op jit(solution)/shard_map/ppermute | solution.py:33
  37.8 23.7 %collective-permute-start.8 = (bf16[64,3072]{1,0:T(8,128)(2,1)}, bf16[64,3072]{1,0:T(8,128)(2,1)S(1)}, u32[]{:S(2)}, u32[]{:S(2)}) collective-permute-start(bf16[64,3072]{1,0:T(8,128)(2,1)} %copy-done.13), channel_id=1, source_target_pairs={{0,3},{1,2},{2,1},{3,0},{4,7},{5,6},{6,5},{7,4},{8,11},{9,10},{10,... | collective-permute-start | bytes 1179656 | tf_op jit(solution)/shard_map/ppermute | solution.py:33
  37.8 1.0 copy-start.16
  49.9 0.7 copy-start.17
  50.6 14.0 %collective-permute-start.12 = (bf16[64,2048]{1,0:T(8,128)(2,1)}, bf16[64,2048]{1,0:T(8,128)(2,1)S(1)}, u32[]{:S(2)}, u32[]{:S(2)}) collective-permute-start(bf16[64,2048]{1,0:T(8,128)(2,1)} %get-tuple-element.37), channel_id=1, source_target_pairs={{0,1},{1,0},{2,3},{3,2},{4,5},{5,4},{6,7},{7,6},{8,9},{9,8},{10,11... | collective-permute-start | bytes 786440 | tf_op jit(solution)/shard_map/ppermute | solution.py:33
  52.0 15.8 %collective-permute-start.13 = (bf16[64,2048]{1,0:T(8,128)(2,1)}, bf16[64,2048]{1,0:T(8,128)(2,1)S(1)}, u32[]{:S(2)}, u32[]{:S(2)}) collective-permute-start(bf16[64,2048]{1,0:T(8,128)(2,1)} %get-tuple-element.38), channel_id=1, source_target_pairs={{0,2},{1,3},{2,0},{3,1},{4,6},{5,7},{6,4},{7,5},{8,10},{9,11},{10,... | collective-permute-start | bytes 786440 | tf_op jit(solution)/shard_map/ppermute | solution.py:33
  52.7 20.0 %collective-permute-start.14 = (bf16[64,2048]{1,0:T(8,128)(2,1)}, bf16[64,2048]{1,0:T(8,128)(2,1)S(1)}, u32[]{:S(2)}, u32[]{:S(2)}) collective-permute-start(bf16[64,2048]{1,0:T(8,128)(2,1)} %copy-done.17), channel_id=1, source_target_pairs={{0,3},{1,2},{2,1},{3,0},{4,7},{5,6},{6,5},{7,4},{8,11},{9,10},{10,... | collective-permute-start | bytes 786440 | tf_op jit(solution)/shard_map/ppermute | solution.py:33
  57.0 21.0 %collective-permute-start.15 = (bf16[64,3072]{1,0:T(8,128)(2,1)}, bf16[64,3072]{1,0:T(8,128)(2,1)S(1)}, u32[]{:S(2)}, u32[]{:S(2)}) collective-permute-start(bf16[64,3072]{1,0:T(8,128)(2,1)} %get-tuple-element.40), channel_id=1, source_target_pairs={{0,1},{1,0},{2,3},{3,2},{4,5},{5,4},{6,7},{7,6},{8,9},{9,8},{10,11... | collective-permute-start | bytes 1179656 | tf_op jit(solution)/shard_map/ppermute | solution.py:33
  64.1 10.9 %collective-permute-start.18 = (bf16[64,2048]{1,0:T(8,128)(2,1)S(1)}, bf16[64,2048]{1,0:T(8,128)(2,1)S(1)}, u32[]{:S(2)}, u32[]{:S(2)}) collective-permute-start(bf16[64,2048]{1,0:T(8,128)(2,1)S(1)} %get-tuple-element.43), channel_id=1, source_target_pairs={{0,1},{1,0},{2,3},{3,2},{4,5},{5,4},{6,7},{7,6},{8,9},{9,8},{10,11... | collective-permute-start | bytes 786440 | tf_op jit(solution)/shard_map/ppermute | solution.py:33
  64.6 0.7 copy-start.1
  65.3 16.6 %collective-permute-start.16 = (bf16[64,3072]{1,0:T(8,128)(2,1)}, bf16[64,3072]{1,0:T(8,128)(2,1)S(1)}, u32[]{:S(2)}, u32[]{:S(2)}) collective-permute-start(bf16[64,3072]{1,0:T(8,128)(2,1)} %get-tuple-element.41), channel_id=1, source_target_pairs={{0,2},{1,3},{2,0},{3,1},{4,6},{5,7},{6,4},{7,5},{8,10},{9,11},{10,... | collective-permute-start | bytes 1179656 | tf_op jit(solution)/shard_map/ppermute | solution.py:33
  67.8 0.7 copy-start.3
  68.5 21.1 %collective-permute-start.17 = (bf16[64,3072]{1,0:T(8,128)(2,1)}, bf16[64,3072]{1,0:T(8,128)(2,1)S(1)}, u32[]{:S(2)}, u32[]{:S(2)}) collective-permute-start(bf16[64,3072]{1,0:T(8,128)(2,1)} %get-tuple-element.42), channel_id=1, source_target_pairs={{0,3},{1,2},{2,1},{3,0},{4,7},{5,6},{6,5},{7,4},{8,11},{9,10},{10,... | collective-permute-start | bytes 1179656 | tf_op jit(solution)/shard_map/ppermute | solution.py:33
  72.8 0.7 copy-start.5
  73.5 22.5 %collective-permute-start.19 = (bf16[64,2048]{1,0:T(8,128)(2,1)}, bf16[64,2048]{1,0:T(8,128)(2,1)}, u32[]{:S(2)}, u32[]{:S(2)}) collective-permute-start(bf16[64,2048]{1,0:T(8,128)(2,1)} %get-tuple-element.44), channel_id=1, source_target_pairs={{0,2},{1,3},{2,0},{3,1},{4,6},{5,7},{6,4},{7,5},{8,10},{9,11},{10,... | collective-permute-start | bytes 786440 | tf_op jit(solution)/shard_map/ppermute | solution.py:33
  75.0 0.7 copy-start.7
  75.7 25.3 %collective-permute-start.20 = (bf16[64,2048]{1,0:T(8,128)(2,1)}, bf16[64,2048]{1,0:T(8,128)(2,1)}, u32[]{:S(2)}, u32[]{:S(2)}) collective-permute-start(bf16[64,2048]{1,0:T(8,128)(2,1)} %get-tuple-element.45), channel_id=1, source_target_pairs={{0,3},{1,2},{2,1},{3,0},{4,7},{5,6},{6,5},{7,4},{8,11},{9,10},{10,... | collective-permute-start | bytes 786440 | tf_op jit(solution)/shard_map/ppermute | solution.py:33
  76.0 15.2 %copy-start.2 = (bf16[64,2048]{1,0:T(8,128)(2,1)S(1)}, bf16[64,2048]{1,0:T(8,128)(2,1)}, u32[]{:S(2)}) copy-start(bf16[64,2048]{1,0:T(8,128)(2,1)} %copy-done.1) | copy-start | bytes 786436
  76.0 15.2 %copy-start.4 = (bf16[64,2048]{1,0:T(8,128)(2,1)S(1)}, bf16[64,2048]{1,0:T(8,128)(2,1)}, u32[]{:S(2)}) copy-start(bf16[64,2048]{1,0:T(8,128)(2,1)} %copy-done.3) | copy-start | bytes 786436
  76.0 15.2 %copy-start.6 = (bf16[64,2048]{1,0:T(8,128)(2,1)S(1)}, bf16[64,2048]{1,0:T(8,128)(2,1)}, u32[]{:S(2)}) copy-start(bf16[64,2048]{1,0:T(8,128)(2,1)} %copy-done.5) | copy-start | bytes 786436
  78.0 24.9 %collective-permute-start.21 = (bf16[64,1024]{1,0:T(8,128)(2,1)S(1)}, bf16[64,1024]{1,0:T(8,128)(2,1)S(1)}, u32[]{:S(2)}, u32[]{:S(2)}) collective-permute-start(bf16[64,1024]{1,0:T(8,128)(2,1)S(1)} %get-tuple-element.46), channel_id=1, source_target_pairs={{0,1},{1,0},{2,3},{3,2},{4,5},{5,4},{6,7},{7,6},{8,9},{9,8},{10,11... | collective-permute-start | bytes 393224 | tf_op jit(solution)/shard_map/ppermute | solution.py:33
  81.9 22.5 %collective-permute-start.22 = (bf16[64,1024]{1,0:T(8,128)(2,1)S(1)}, bf16[64,1024]{1,0:T(8,128)(2,1)S(1)}, u32[]{:S(2)}, u32[]{:S(2)}) collective-permute-start(bf16[64,1024]{1,0:T(8,128)(2,1)S(1)} %get-tuple-element.47), channel_id=1, source_target_pairs={{0,2},{1,3},{2,0},{3,1},{4,6},{5,7},{6,4},{7,5},{8,10},{9,11},{10,... | collective-permute-start | bytes 393224 | tf_op jit(solution)/shard_map/ppermute | solution.py:33
  89.6 16.9 %collective-permute-start.23 = (bf16[64,1024]{1,0:T(8,128)(2,1)S(1)}, bf16[64,1024]{1,0:T(8,128)(2,1)S(1)}, u32[]{:S(2)}, u32[]{:S(2)}) collective-permute-start(bf16[64,1024]{1,0:T(8,128)(2,1)S(1)} %get-tuple-element.48), channel_id=1, source_target_pairs={{0,3},{1,2},{2,1},{3,0},{4,7},{5,6},{6,5},{7,4},{8,11},{9,10},{10,... | collective-permute-start | bytes 393224 | tf_op jit(solution)/shard_map/ppermute | solution.py:33
  92.1 8.8 %copy-start.8 = (bf16[64,2048]{1,0:T(8,128)(2,1)S(1)}, bf16[64,2048]{1,0:T(8,128)(2,1)}, u32[]{:S(2)}) copy-start(bf16[64,2048]{1,0:T(8,128)(2,1)} %copy-done.7) | copy-start | bytes 786436
where the time goes:
time: 108 us; the launch traced here: 107 us
  Pallas kernels  44.5 us (41%)
  waiting for transfers between devices  30 us (28%)
  starting transfers between devices  26.4 us (24%)
  local copies, waits for them, and re-layouts  5.98 us (6%)
    ppermute x20, waiting for transfers between devices, swap(): return lax.ppermute(array, 'narrow', [(i, i ^ d) for i in range(n)])  28.7 us
    ppermute x20, starting transfers between devices, swap(): return lax.ppermute(array, 'narrow', [(i, i ^ d) for i in range(n)])  18 us
    pallas_call x4, Pallas kernels, apply(): pl.pallas_call(functools.partial(apply_kernel, parts), grid_spec=pltpu.Pr...  10.8 us
    pallas_call x1, Pallas kernels, transform(): pl.pallas_call(transform_kernel, grid=(1,), in_specs=[pl.BlockSpec((used,...  8.54 us
    pallas_call x5, Pallas kernels, pack(): pl.pallas_call(functools.partial(pack_kernel, partners, cells, start), in...  7.81 us
    pallas_call x1, Pallas kernels, gather(): pl.pallas_call(functools.partial(gather_kernel, regions), in_specs=[SMEM]...  7.65 us
    unnamed x36, local copies, waits for them, and re-layouts  5.98 us
    pallas_call x5, Pallas kernels, place(): pl.pallas_call(functools.partial(place_kernel, cells, start, partners), i...  5.26 us
  transfers between devices with their start and end apart: 24, of which 10 were waited for; matrix products, arithmetic and copies ran while one was open for 0% of the time, Pallas kernels for 41%

commit v1 on v0

--- a/solution.py
+++ b/solution.py
@@ -10,9 +10,9 @@
 HALO = 256
 ITERS = 6
 LANES = 128
-FIRST = [(0, 2), (2, 3), (5, 3)]
-OTHERS = [(0, 5), (5, 3)]
-STEPS = [(0, 2), (2, 3), (5, 2), (7, 1)]
+FIRST = [(0, 2), (2, 2), (4, 4)]
+OTHERS = [(0, 4), (4, 4)]
+STEPS = [(0, 2), (2, 2), (4, 3), (7, 1)]
 
 
 VMEM = pl.BlockSpec(memory_space=pltpu.VMEM)
@@ -252,8 +252,7 @@
     )(picked, stat, *others)
 
 
-def apply_kernel(parts, at_ref, weights_ref, *refs):
-    del at_ref
+def apply_kernel(parts, weights_ref, *refs):
     sources, outs = refs[:parts], refs[-parts:]
     pieces = [r[...].astype(jnp.float32) for r in sources]
     rows = pieces[0].shape[0]
@@ -266,34 +265,33 @@
         outs[d][...] = result[d * rows : (d + 1) * rows]
 
 
-def apply(weights, states, arrived, offsets, result, at, blocks, block):
+def apply(weights, states, arrived, offsets, result, first, blocks, block, stride):
     rows = states.shape[0]
     width = blocks * block
     parts = len(arrived) + 1
     members = rows * parts
 
     def far(offset):
-        return pl.BlockSpec((rows, block), lambda i, at: (0, offset + i))
-
-    near = pl.BlockSpec((rows, block), lambda i, at: (0, at[0] + i))
+        return pl.BlockSpec((rows, block), lambda i: (0, offset + i))
+
+    near = pl.BlockSpec(
+        (rows, block), lambda i: (0, lax.axis_index("narrow") * stride + first + i)
+    )
     given = [] if result is None else [result]
     return pl.pallas_call(
         functools.partial(apply_kernel, parts),
-        grid_spec=pltpu.PrefetchScalarGridSpec(
-            num_scalar_prefetch=1,
-            grid=(blocks,),
-            in_specs=[pl.BlockSpec((members, members), lambda i, at: (0, 0)), near]
-            + [far(offset) for offset in offsets]
-            + [HBM] * len(given),
-            out_specs=[near] + [far(0)] * (parts - 1),
-        ),
+        grid=(blocks,),
+        in_specs=[pl.BlockSpec((members, members), lambda i: (0, 0)), near]
+        + [far(offset) for offset in offsets]
+        + [HBM] * len(given),
+        out_specs=[near] + [far(0)] * (parts - 1),
         out_shape=[jax.ShapeDtypeStruct(states.shape, jnp.bfloat16)]
-        + [jax.ShapeDtypeStruct((rows, width), jnp.bfloat16)] * (parts - 1),
-        input_output_aliases={2 + parts: 0} if given else {},
+        + [pltpu.VMEM((rows, width), jnp.bfloat16)] * (parts - 1),
+        input_output_aliases={1 + parts: 0} if given else {},
         compiler_params=params(),
         cost_estimate=cost(2 * members * members * width, 4 * members * width),
         name="apply",
-    )(at, weights, states, *arrived, *given)
+    )(weights, states, *arrived, *given)
 
 
 def place_kernel(cells, start, partners, result_ref, *refs):
@@ -327,7 +325,6 @@
 
 def body(states, obs_ens, obs_value, obs_prec, obs_pick, taper):
     n = lax.axis_size("narrow")
-    pos = lax.axis_index("narrow")
     cells = states.shape[1] // n
     unit = cells // 8
     states = pltpu.with_memory_space_constraint(states, pltpu.HBM)
@@ -361,14 +358,15 @@
 
     result, outgoing = None, []
     for first, count in STEPS:
-        at = jnp.reshape((pos * cells) // unit + first, (1,))
         parts, offsets = [], []
         for d in range(1, n):
             for base, units, part in arrived[d]:
                 if base <= first < base + units:
                     parts.append(part)
                     offsets.append(first - base)
-        result, *leaving = apply(weights, states, parts, offsets, result, at, count, unit)
+        result, *leaving = apply(
+            weights, states, parts, offsets, result, first, count, unit, cells // unit
+        )
         moved = []
         for d, part in enumerate(leaving, 1):
             moved.append(swap(part, d))

time: 108 us -> 123 us (1.14)
  waiting for transfers between devices: 30 us -> 59 us
  local copies, waits for them, and re-layouts: 5.98 us -> 0.02 us
  Pallas kernels: 44.5 us -> 38.9 us
  starting transfers between devices: 26.4 us -> 25 us
    ppermute x20, waiting for transfers between devices: 28.7 us -> 55.4 us  [swap(): return lax.ppermute(array, 'narrow', [(i, i ^ d) for i in range(n)])]
    unnamed x36 -> x10, local copies, waits for them, and re-layouts: 5.98 us -> 0.02 us
    ppermute x2, waiting for transfers between devices: 0.01 us -> 2.46 us  [halo(): after = lax.ppermute(first, ('wide', 'narrow'), down)]
    pallas_call x5, Pallas kernels: 7.81 us -> 5.42 us  [pack(): pl.pallas_call(functools.partial(pack_kernel, partners, cells, start), in...]
    ppermute x20, starting transfers between devices: 18 us -> 16.6 us  [swap(): return lax.ppermute(array, 'narrow', [(i, i ^ d) for i in range(n)])]
  transfers between devices with their start and end apart: 24 -> 24, of which waited for: 10 -> 10; matrix products, arithmetic and copies ran while one was open for 0% -> 0% of each run, Pallas kernels for 41% -> 31%
where the time goes in v1:
time: 123 us
  waiting for transfers between devices  59 us (48%)
  Pallas kernels  38.9 us (32%)
  starting transfers between devices  25 us (20%)
    ppermute x20, waiting for transfers between devices, swap(): return lax.ppermute(array, 'narrow', [(i, i ^ d) for i in range(n)])  55.4 us
    ppermute x20, starting transfers between devices, swap(): return lax.ppermute(array, 'narrow', [(i, i ^ d) for i in range(n)])  16.6 us
    pallas_call x4, Pallas kernels, apply(): pl.pallas_call(functools.partial(apply_kernel, parts), grid=(blocks,), in...  10.3 us
    pallas_call x1, Pallas kernels, transform(): pl.pallas_call(transform_kernel, grid=(1,), in_specs=[pl.BlockSpec((used,...  7.59 us
    pallas_call x1, Pallas kernels, gather(): pl.pallas_call(functools.partial(gather_kernel, regions), in_specs=[SMEM]...  6.91 us
    pallas_call x5, Pallas kernels, pack(): pl.pallas_call(functools.partial(pack_kernel, partners, cells, start), in...  5.42 us
    pallas_call x1, Pallas kernels, stats(): pl.pallas_call(stats_kernel, in_specs=[SMEM] + [VMEM] * (1 + len(parts)),...  4.47 us
    ppermute x2, starting transfers between devices, halo(): after = lax.ppermute(first, ('wide', 'narrow'), down)  4.25 us
  transfers between devices with their start and end apart: 24, of which 10 were waited for; matrix products, arithmetic and copies ran while one was open for 0% of the time, Pallas kernels for 31%

profile of v1, /device:TPU:0, one launch (start us, length us, event | category | flops | bytes accessed | tf_op | source)
XLA Modules:
  0.0 123.1 jit_solution(9131051960890628387)
XLA Ops:
  0.0 0.6 collective-permute-start.2
  0.6 1.2 %pack.5 = bf16[64,8192]{1,0:T(8,128)(2,1)S(1)} custom-call(bf16[64,32768]{1,0:T(8,128)(2,1)} %refs_0_.9), custom_call_target="tpu_custom_call" | custom-call | bytes 2097152 | tf_op jit(solution)/shard_map/pack/pallas_call | solution.py:64
  1.8 0.1 collective-permute-start.6
  2.0 2.6 %collective-permute-start.1 = (f32[72,256]{1,0:T(8,128)S(1)}, f32[72,256]{1,0:T(8,128)S(1)}, u32[]{:S(2)}, u32[]{:S(2)}) collective-permute-start(f32[72,256]{1,0:T(8,128)S(1)} %get-tuple-element.27), channel_id=1, source_target_pairs={{0,5},{1,4},{2,7},{3,6},{4,9},{5,8},{6,11},{7,10},{8,13},{9,12},{1... | collective-permute-start | bytes 221192 | tf_op jit(solution)/shard_map/ppermute | solution.py:40
  4.6 1.5 %collective-permute-start = (f32[72,256]{1,0:T(8,128)S(1)}, f32[72,256]{1,0:T(8,128)S(1)}, u32[]{:S(2)}, u32[]{:S(2)}) collective-permute-start(f32[72,256]{1,0:T(8,128)S(1)} %get-tuple-element.27), channel_id=1, source_target_pairs={{0,4},{1,5},{2,6},{3,7},{4,8},{5,9},{6,10},{7,11},{8,12},{9,13},{1... | collective-permute-start | bytes 221192 | tf_op jit(solution)/shard_map/ppermute | solution.py:40
  6.2 1.0 pack.9
  7.1 1.6 %collective-permute-start.11 = (bf16[64,2048]{1,0:T(8,128)(2,1)S(1)}, bf16[64,2048]{1,0:T(8,128)(2,1)S(1)}, u32[]{:S(2)}, u32[]{:S(2)}) collective-permute-start(bf16[64,2048]{1,0:T(8,128)(2,1)S(1)} %pack.9), channel_id=1, source_target_pairs={{0,2},{1,3},{2,0},{3,1},{4,6},{5,7},{6,4},{7,5},{8,10},{9,11},{10,... | collective-permute-start | bytes 786440 | tf_op jit(solution)/shard_map/ppermute | solution.py:33
  8.7 1.2 collective-permute-done.1.refs_1_
  9.9 2.4 %collective-permute-start.4 = (f32[72,256]{1,0:T(8,128)S(1)}, f32[72,256]{1,0:T(8,128)S(1)}, u32[]{:S(2)}, u32[]{:S(2)}) collective-permute-start(f32[72,256]{1,0:T(8,128)S(1)} %get-tuple-element.28), channel_id=1, source_target_pairs={{0,29},{1,28},{2,31},{3,30},{4,1},{5,0},{6,3},{7,2},{8,5},{9,4},{1... | collective-permute-start | bytes 221192 | tf_op jit(solution)/shard_map/ppermute | solution.py:41
  12.2 0.0 collective-permute-done.refs_0_.before_ref
  12.2 1.9 %collective-permute-start.3 = (f32[72,256]{1,0:T(8,128)S(1)}, f32[72,256]{1,0:T(8,128)S(1)}, u32[]{:S(2)}, u32[]{:S(2)}) collective-permute-start(f32[72,256]{1,0:T(8,128)S(1)} %get-tuple-element.28), channel_id=1, source_target_pairs={{0,28},{1,29},{2,30},{3,31},{4,0},{5,1},{6,2},{7,3},{8,4},{9,5},{1... | collective-permute-start | bytes 221192 | tf_op jit(solution)/shard_map/ppermute | solution.py:41
  14.1 0.5 collective-permute-done.4.refs_5_
  14.7 1.9 %collective-permute-done.3.refs_4_.after_ref = f32[72,256]{1,0:T(8,128)S(1)} collective-permute-done((f32[72,256]{1,0:T(8,128)S(1)}, f32[72,256]{1,0:T(8,128)S(1)}, u32[]{:S(2)}, u32[]{:S(2)}) %collective-permute-start.3) | collective-permute-done | bytes 73760 | tf_op jit(solution)/shard_map/ppermute | solution.py:41
  16.6 0.0 collective-permute-done.2.refs_3_
  16.6 6.9 %gather.1 = (bf16[1024,128]{1,0:T(8,128)(2,1)S(1)}, bf16[1024,128]{1,0:T(8,128)(2,1)S(1)}) custom-call(s32[4,1024]{1,0:T(4,128)S(1)} %copy-done.3, f32[72,256]{1,0:T(8,128)S(1)} %collective-permute-done.refs_0_.before_ref, f32[72,256]{1,0:T(8,128)S(1)} %collective-permute-done.1.refs_1_, bf16[64,4096]{1,0:T(8,128)(2,1)S(1)} %copy-done, ...), custom_call_target="tpu_custom_call" | custom-call | bytes 6815744 | tf_op jit(solution)/shard_map/gather/pallas_call | solution.py:141
  23.5 1.6 %collective-permute-start.5 = (bf16[1024,128]{1,0:T(8,128)(2,1)S(1)}, bf16[1024,128]{1,0:T(8,128)(2,1)S(1)}, u32[]{:S(2)}, u32[]{:S(2)}) collective-permute-start(bf16[1024,128]{1,0:T(8,128)(2,1)S(1)} %get-tuple-element.30), channel_id=1, source_target_pairs={{0,2},{1,3},{2,0},{3,1},{4,6},{5,7},{6,4},{7,5},{8,10},{9,11},{10,... | collective-permute-start | bytes 786440 | tf_op jit(solution)/shard_map/ppermute | solution.py:33
  25.2 1.0 pack.8
  26.2 0.0 copy-start.4
  26.2 0.1 collective-permute-start.10
  26.3 1.2 pack.6
  27.5 0.5 collective-permute-start.7
  28.1 0.0 collective-permute-done.11.refs_2_
  28.1 1.4 %collective-permute-start.8 = (bf16[64,4096]{1,0:T(8,128)(2,1)S(1)}, bf16[64,4096]{1,0:T(8,128)(2,1)S(1)}, u32[]{:S(2)}, u32[]{:S(2)}) collective-permute-start(bf16[64,4096]{1,0:T(8,128)(2,1)S(1)} %get-tuple-element.32), channel_id=1, source_target_pairs={{0,3},{1,2},{2,1},{3,0},{4,7},{5,6},{6,5},{7,4},{8,11},{9,10},{10,... | collective-permute-start | bytes 1572872 | tf_op jit(solution)/shard_map/ppermute | solution.py:33
  29.5 1.0 pack.7
  30.5 4.5 %stats.1.stats_ref = f32[1024,8]{1,0:T(8,128)S(1)} custom-call(s32[4,1024]{1,0:T(4,128)S(1)} %copy-done.3, f32[1,1024]{1,0:T(1,128)S(1)} %copy-done.4, f32[72,256]{1,0:T(8,128)S(1)} %collective-permute-done.refs_0_.before_ref, f32[1,4096]{1,0:T(1,128)S(1)} %bitcast.4, f32[1,4096]{1,0:T(1,128)S(1)} %bitcast.7, ...), custom_call_target="tpu_custom_call" | custom-call | bytes 2883584 | tf_op jit(solution)/shard_map/stats/pallas_call | solution.py:189
  35.0 0.0 collective-permute-done.5.refs_0_
  35.0 1.6 %collective-permute-start.9 = (bf16[64,2048]{1,0:T(8,128)(2,1)S(1)}, bf16[64,2048]{1,0:T(8,128)(2,1)S(1)}, u32[]{:S(2)}, u32[]{:S(2)}) collective-permute-start(bf16[64,2048]{1,0:T(8,128)(2,1)S(1)} %pack.7), channel_id=1, source_target_pairs={{0,2},{1,3},{2,0},{3,1},{4,6},{5,7},{6,4},{7,5},{8,10},{9,11},{10,... | collective-permute-start | bytes 786440 | tf_op jit(solution)/shard_map/ppermute | solution.py:33
  36.6 7.6 %transform.1.weights_ref = bf16[256,256]{1,0:T(8,128)(2,1)S(1)} custom-call(bf16[1024,128]{1,0:T(8,128)(2,1)S(1)} %get-tuple-element.29.own_ref, f32[1024,8]{1,0:T(8,128)S(1)} %stats.1.stats_ref, bf16[1024,128]{1,0:T(8,128)(2,1)S(1)} %collective-permute-done.5.refs_0_), custom_call_target="tpu_custom_call" | custom-call | flops 3221225472 | bytes 1048576 | tf_op jit(solution)/shard_map/transform/pallas_call | solution.py:239
  44.2 0.0 collective-permute-done.10.refs_3_
  44.2 0.0 collective-permute-done.6.refs_1_
  44.2 2.5 %apply.4 = (bf16[64,32768]{1,0:T(8,128)(2,1)}, bf16[64,2048]{1,0:T(8,128)(2,1)S(1)}, bf16[64,2048]{1,0:T(8,128)(2,1)S(1)}, bf16[64,2048]{1,0:T(8,128)(2,1)S(1)}) custom-call(bf16[256,256]{1,0:T(8,128)(2,1)S(1)} %transform.1.weights_ref, bf16[64,32768]{1,0:T(8,128)(2,1)} %refs_0_.9, bf16[64,8192]{1,0:T(8,128)(2,1)S(1)} %collective-permute-done.6.refs_1_, ...), custom_call_target="tpu_custom_call" | custom-call | flops 268435456 | bytes 2097152 | tf_op jit(solution)/shard_map/apply/pallas_call | solution.py:281
  46.7 23.5 %collective-permute-done.9.refs_2_ = bf16[64,2048]{1,0:T(8,128)(2,1)S(1)} collective-permute-done((bf16[64,2048]{1,0:T(8,128)(2,1)S(1)}, bf16[64,2048]{1,0:T(8,128)(2,1)S(1)}, u32[]{:S(2)}, u32[]{:S(2)}) %collective-permute-start.9) | collective-permute-done | bytes 262176 | tf_op jit(solution)/shard_map/ppermute | solution.py:33
  70.2 2.5 %apply.5 = (bf16[64,32768]{1,0:T(8,128)(2,1)}, bf16[64,2048]{1,0:T(8,128)(2,1)S(1)}, bf16[64,2048]{1,0:T(8,128)(2,1)S(1)}, bf16[64,2048]{1,0:T(8,128)(2,1)S(1)}) custom-call(bf16[256,256]{1,0:T(8,128)(2,1)S(1)} %transform.1.weights_ref, bf16[64,32768]{1,0:T(8,128)(2,1)} %refs_0_.9, ...), custom_call_target="tpu_custom_call", output_to_operand_aliasing={{0}: (5, {})} | custom-call | flops 268435456 | bytes 2097152 | tf_op jit(solution)/shard_map/apply/pallas_call | solution.py:281
  72.7 0.0 collective-permute-start.15
  72.7 1.5 %collective-permute-start.16 = (bf16[64,2048]{1,0:T(8,128)(2,1)S(1)}, bf16[64,2048]{1,0:T(8,128)(2,1)S(1)}, u32[]{:S(2)}, u32[]{:S(2)}) collective-permute-start(bf16[64,2048]{1,0:T(8,128)(2,1)S(1)} %get-tuple-element.41), channel_id=1, source_target_pairs={{0,2},{1,3},{2,0},{3,1},{4,6},{5,7},{6,4},{7,5},{8,10},{9,11},{10,... | collective-permute-start | bytes 786440 | tf_op jit(solution)/shard_map/ppermute | solution.py:33
  74.2 0.3 collective-permute-start.17
  74.5 0.0 collective-permute-done.7.refs_2_
  74.5 0.3 collective-permute-start.12
  74.8 0.0 collective-permute-done.8.refs_3_
  74.8 3.4 %apply.6 = (bf16[64,32768]{1,0:T(8,128)(2,1)}, bf16[64,3072]{1,0:T(8,128)(2,1)S(1)}, bf16[64,3072]{1,0:T(8,128)(2,1)S(1)}, bf16[64,3072]{1,0:T(8,128)(2,1)S(1)}) custom-call(bf16[256,256]{1,0:T(8,128)(2,1)S(1)} %transform.1.weights_ref, bf16[64,32768]{1,0:T(8,128)(2,1)} %refs_0_.9, ...), custom_call_target="tpu_custom_call", output_to_operand_aliasing={{0}: (5, {})} | custom-call | flops 402653184 | bytes 3145728 | tf_op jit(solution)/shard_map/apply/pallas_call | solution.py:281
  78.2 0.2 collective-permute-start.18
  78.4 0.0 collective-permute-done.15.refs_0_
  78.4 1.5 %collective-permute-start.13 = (bf16[64,2048]{1,0:T(8,128)(2,1)S(1)}, bf16[64,2048]{1,0:T(8,128)(2,1)S(1)}, u32[]{:S(2)}, u32[]{:S(2)}) collective-permute-start(bf16[64,2048]{1,0:T(8,128)(2,1)S(1)} %get-tuple-element.38), channel_id=1, source_target_pairs={{0,2},{1,3},{2,0},{3,1},{4,6},{5,7},{6,4},{7,5},{8,10},{9,11},{10,... | collective-permute-start | bytes 786440 | tf_op jit(solution)/shard_map/ppermute | solution.py:33
  79.9 1.9 %collective-permute-done.16.refs_1_ = bf16[64,2048]{1,0:T(8,128)(2,1)S(1)} collective-permute-done((bf16[64,2048]{1,0:T(8,128)(2,1)S(1)}, bf16[64,2048]{1,0:T(8,128)(2,1)S(1)}, u32[]{:S(2)}, u32[]{:S(2)}) %collective-permute-start.16) | collective-permute-done | bytes 262176 | tf_op jit(solution)/shard_map/ppermute | solution.py:33
  81.8 1.5 %collective-permute-start.19 = (bf16[64,3072]{1,0:T(8,128)(2,1)S(1)}, bf16[64,3072]{1,0:T(8,128)(2,1)S(1)}, u32[]{:S(2)}, u32[]{:S(2)}) collective-permute-start(bf16[64,3072]{1,0:T(8,128)(2,1)S(1)} %get-tuple-element.44), channel_id=1, source_target_pairs={{0,2},{1,3},{2,0},{3,1},{4,6},{5,7},{6,4},{7,5},{8,10},{9,11},{10,... | collective-permute-start | bytes 1179656 | tf_op jit(solution)/shard_map/ppermute | solution.py:33
  83.4 3.2 %collective-permute-done.17.refs_2_ = bf16[64,2048]{1,0:T(8,128)(2,1)S(1)} collective-permute-done((bf16[64,2048]{1,0:T(8,128)(2,1)S(1)}, bf16[64,2048]{1,0:T(8,128)(2,1)S(1)}, u32[]{:S(2)}, u32[]{:S(2)}) %collective-permute-start.17) | collective-permute-done | bytes 262176 | tf_op jit(solution)/shard_map/ppermute | solution.py:33
  86.5 1.9 %collective-permute-start.20 = (bf16[64,3072]{1,0:T(8,128)(2,1)S(1)}, bf16[64,3072]{1,0:T(8,128)(2,1)S(1)}, u32[]{:S(2)}, u32[]{:S(2)}) collective-permute-start(bf16[64,3072]{1,0:T(8,128)(2,1)S(1)} %get-tuple-element.45), channel_id=1, source_target_pairs={{0,3},{1,2},{2,1},{3,0},{4,7},{5,6},{6,5},{7,4},{8,11},{9,10},{10,... | collective-permute-start | bytes 1179656 | tf_op jit(solution)/shard_map/ppermute | solution.py:33
  88.4 0.0 collective-permute-done.12.refs_0_
  88.4 0.0 collective-permute-start.14
  88.5 1.9 %apply.7 = (bf16[64,32768]{1,0:T(8,128)(2,1)}, bf16[64,1024]{1,0:T(8,128)(2,1)S(1)}, bf16[64,1024]{1,0:T(8,128)(2,1)S(1)}, bf16[64,1024]{1,0:T(8,128)(2,1)S(1)}) custom-call(bf16[256,256]{1,0:T(8,128)(2,1)S(1)} %transform.1.weights_ref, bf16[64,32768]{1,0:T(8,128)(2,1)} %refs_0_.9, ...), custom_call_target="tpu_custom_call", output_to_operand_aliasing={{0}: (5, {})} | custom-call | flops 134217728 | bytes 1048576 | tf_op jit(solution)/shard_map/apply/pallas_call | solution.py:281
  90.4 2.7 %collective-permute-done.13.refs_1_ = bf16[64,2048]{1,0:T(8,128)(2,1)S(1)} collective-permute-done((bf16[64,2048]{1,0:T(8,128)(2,1)S(1)}, bf16[64,2048]{1,0:T(8,128)(2,1)S(1)}, u32[]{:S(2)}, u32[]{:S(2)}) %collective-permute-start.13) | collective-permute-done | bytes 262176 | tf_op jit(solution)/shard_map/ppermute | solution.py:33
  93.1 21.5 %collective-permute-done.14.refs_2_ = bf16[64,2048]{1,0:T(8,128)(2,1)S(1)} collective-permute-done((bf16[64,2048]{1,0:T(8,128)(2,1)S(1)}, bf16[64,2048]{1,0:T(8,128)(2,1)S(1)}, u32[]{:S(2)}, u32[]{:S(2)}) %collective-permute-start.14) | collective-permute-done | bytes 262176 | tf_op jit(solution)/shard_map/ppermute | solution.py:33
  114.6 1.5 %collective-permute-start.22 = (bf16[64,1024]{1,0:T(8,128)(2,1)S(1)}, bf16[64,1024]{1,0:T(8,128)(2,1)S(1)}, u32[]{:S(2)}, u32[]{:S(2)}) collective-permute-start(bf16[64,1024]{1,0:T(8,128)(2,1)S(1)} %get-tuple-element.47), channel_id=1, source_target_pairs={{0,2},{1,3},{2,0},{3,1},{4,6},{5,7},{6,4},{7,5},{8,10},{9,11},{10,... | collective-permute-start | bytes 393224 | tf_op jit(solution)/shard_map/ppermute | solution.py:33
  116.2 0.0 collective-permute-done.18.refs_0_
  116.2 0.1 collective-permute-start.23
  116.3 0.9 place.5.result_ref
  117.2 0.9 place.6.result_ref
  118.1 0.0 collective-permute-done.19.refs_1_
  118.1 1.0 place.7.result_ref
  119.2 0.0 collective-permute-done.21.refs_0_
  119.2 1.8 %collective-permute-done.22.refs_1_ = bf16[64,1024]{1,0:T(8,128)(2,1)S(1)} collective-permute-done((bf16[64,1024]{1,0:T(8,128)(2,1)S(1)}, bf16[64,1024]{1,0:T(8,128)(2,1)S(1)}, u32[]{:S(2)}, u32[]{:S(2)}) %collective-permute-start.22) | collective-permute-done | bytes 131104 | tf_op jit(solution)/shard_map/ppermute | solution.py:33
  121.0 0.7 place.8.result_ref
  121.7 0.7 collective-permute-done.23.refs_0_
  122.4 0.7 place.9
  (12 shorter events, 0.0 us)
Async XLA Ops:
  0.0 2.0 %copy-start = (bf16[64,4096]{1,0:T(8,128)(2,1)S(1)}, bf16[64,4096]{1,0:T(8,128)(2,1)}, u32[]{:S(2)}) copy-start(bf16[64,4096]{1,0:T(8,128)(2,1)} %refs_2_.1) | copy-start | bytes 1572868
  0.0 2.0 %copy-start.2 = (f32[4096]{0:T(1024)S(1)}, f32[4096]{0:T(1024)}, u32[]{:S(2)}) copy-start(f32[4096]{0:T(1024)} %param.9) | copy-start | bytes 49156
  0.0 2.0 %copy-start.1 = (f32[4096]{0:T(1024)S(1)}, f32[4096]{0:T(1024)}, u32[]{:S(2)}) copy-start(f32[4096]{0:T(1024)} %param.8) | copy-start | bytes 49156
  0.0 16.6 %copy-start.3 = (s32[4,1024]{1,0:T(4,128)S(1)}, s32[4,1024]{1,0:T(4,128)}, u32[]{:S(2)}) copy-start(s32[4,1024]{1,0:T(4,128)} %pick_ref.3) | copy-start | bytes 49156
  0.0 16.6 %collective-permute-start.2 = (bf16[64,4096]{1,0:T(8,128)(2,1)}, bf16[64,4096]{1,0:T(8,128)(2,1)S(1)}, u32[]{:S(2)}, u32[]{:S(2)}) collective-permute-start(bf16[64,4096]{1,0:T(8,128)(2,1)} %refs_2_.1), channel_id=1, source_target_pairs={{0,1},{1,0},{2,3},{3,2},{4,5},{5,4},{6,7},{7,6},{8,9},{9,8},{10,11... | collective-permute-start | bytes 1572872 | tf_op jit(solution)/shard_map/ppermute | solution.py:33
  1.8 42.4 %collective-permute-start.6 = (bf16[64,8192]{1,0:T(8,128)(2,1)S(1)}, bf16[64,8192]{1,0:T(8,128)(2,1)S(1)}, u32[]{:S(2)}, u32[]{:S(2)}) collective-permute-start(bf16[64,8192]{1,0:T(8,128)(2,1)S(1)} %pack.5), channel_id=1, source_target_pairs={{0,1},{1,0},{2,3},{3,2},{4,5},{5,4},{6,7},{7,6},{8,9},{9,8},{10,11... | collective-permute-start | bytes 3145736 | tf_op jit(solution)/shard_map/ppermute | solution.py:33
  2.0 7.9 %collective-permute-start.1 = (f32[72,256]{1,0:T(8,128)S(1)}, f32[72,256]{1,0:T(8,128)S(1)}, u32[]{:S(2)}, u32[]{:S(2)}) collective-permute-start(f32[72,256]{1,0:T(8,128)S(1)} %get-tuple-element.27), channel_id=1, source_target_pairs={{0,5},{1,4},{2,7},{3,6},{4,9},{5,8},{6,11},{7,10},{8,13},{9,12},{1... | collective-permute-start | bytes 221192 | tf_op jit(solution)/shard_map/ppermute | solution.py:40
  4.6 7.6 %collective-permute-start = (f32[72,256]{1,0:T(8,128)S(1)}, f32[72,256]{1,0:T(8,128)S(1)}, u32[]{:S(2)}, u32[]{:S(2)}) collective-permute-start(f32[72,256]{1,0:T(8,128)S(1)} %get-tuple-element.27), channel_id=1, source_target_pairs={{0,4},{1,5},{2,6},{3,7},{4,8},{5,9},{6,10},{7,11},{8,12},{9,13},{1... | collective-permute-start | bytes 221192 | tf_op jit(solution)/shard_map/ppermute | solution.py:40
  7.1 20.9 %collective-permute-start.11 = (bf16[64,2048]{1,0:T(8,128)(2,1)S(1)}, bf16[64,2048]{1,0:T(8,128)(2,1)S(1)}, u32[]{:S(2)}, u32[]{:S(2)}) collective-permute-start(bf16[64,2048]{1,0:T(8,128)(2,1)S(1)} %pack.9), channel_id=1, source_target_pairs={{0,2},{1,3},{2,0},{3,1},{4,6},{5,7},{6,4},{7,5},{8,10},{9,11},{10,... | collective-permute-start | bytes 786440 | tf_op jit(solution)/shard_map/ppermute | solution.py:33
  9.9 4.8 %collective-permute-start.4 = (f32[72,256]{1,0:T(8,128)S(1)}, f32[72,256]{1,0:T(8,128)S(1)}, u32[]{:S(2)}, u32[]{:S(2)}) collective-permute-start(f32[72,256]{1,0:T(8,128)S(1)} %get-tuple-element.28), channel_id=1, source_target_pairs={{0,29},{1,28},{2,31},{3,30},{4,1},{5,0},{6,3},{7,2},{8,5},{9,4},{1... | collective-permute-start | bytes 221192 | tf_op jit(solution)/shard_map/ppermute | solution.py:41
  12.2 4.4 %collective-permute-start.3 = (f32[72,256]{1,0:T(8,128)S(1)}, f32[72,256]{1,0:T(8,128)S(1)}, u32[]{:S(2)}, u32[]{:S(2)}) collective-permute-start(f32[72,256]{1,0:T(8,128)S(1)} %get-tuple-element.28), channel_id=1, source_target_pairs={{0,28},{1,29},{2,30},{3,31},{4,0},{5,1},{6,2},{7,3},{8,4},{9,5},{1... | collective-permute-start | bytes 221192 | tf_op jit(solution)/shard_map/ppermute | solution.py:41
  23.5 11.4 %collective-permute-start.5 = (bf16[1024,128]{1,0:T(8,128)(2,1)S(1)}, bf16[1024,128]{1,0:T(8,128)(2,1)S(1)}, u32[]{:S(2)}, u32[]{:S(2)}) collective-permute-start(bf16[1024,128]{1,0:T(8,128)(2,1)S(1)} %get-tuple-element.30), channel_id=1, source_target_pairs={{0,2},{1,3},{2,0},{3,1},{4,6},{5,7},{6,4},{7,5},{8,10},{9,11},{10,... | collective-permute-start | bytes 786440 | tf_op jit(solution)/shard_map/ppermute | solution.py:33
  26.2 4.3 %copy-start.4 = (f32[1,1024]{1,0:T(1,128)S(1)}, f32[1,1024]{1,0:T(1,128)}, u32[]{:S(2)}) copy-start(f32[1,1024]{1,0:T(1,128)} %taper_ref.1) | copy-start | bytes 12292
  26.2 18.0 %collective-permute-start.10 = (bf16[64,4096]{1,0:T(8,128)(2,1)S(1)}, bf16[64,4096]{1,0:T(8,128)(2,1)S(1)}, u32[]{:S(2)}, u32[]{:S(2)}) collective-permute-start(bf16[64,4096]{1,0:T(8,128)(2,1)S(1)} %pack.8), channel_id=1, source_target_pairs={{0,3},{1,2},{2,1},{3,0},{4,7},{5,6},{6,5},{7,4},{8,11},{9,10},{10,... | collective-permute-start | bytes 1572872 | tf_op jit(solution)/shard_map/ppermute | solution.py:33
  27.5 47.0 %collective-permute-start.7 = (bf16[64,4096]{1,0:T(8,128)(2,1)S(1)}, bf16[64,4096]{1,0:T(8,128)(2,1)S(1)}, u32[]{:S(2)}, u32[]{:S(2)}) collective-permute-start(bf16[64,4096]{1,0:T(8,128)(2,1)S(1)} %get-tuple-element.31), channel_id=1, source_target_pairs={{0,2},{1,3},{2,0},{3,1},{4,6},{5,7},{6,4},{7,5},{8,10},{9,11},{10,... | collective-permute-start | bytes 1572872 | tf_op jit(solution)/shard_map/ppermute | solution.py:33
  28.1 46.8 %collective-permute-start.8 = (bf16[64,4096]{1,0:T(8,128)(2,1)S(1)}, bf16[64,4096]{1,0:T(8,128)(2,1)S(1)}, u32[]{:S(2)}, u32[]{:S(2)}) collective-permute-start(bf16[64,4096]{1,0:T(8,128)(2,1)S(1)} %get-tuple-element.32), channel_id=1, source_target_pairs={{0,3},{1,2},{2,1},{3,0},{4,7},{5,6},{6,5},{7,4},{8,11},{9,10},{10,... | collective-permute-start | bytes 1572872 | tf_op jit(solution)/shard_map/ppermute | solution.py:33
  35.0 35.2 %collective-permute-start.9 = (bf16[64,2048]{1,0:T(8,128)(2,1)S(1)}, bf16[64,2048]{1,0:T(8,128)(2,1)S(1)}, u32[]{:S(2)}, u32[]{:S(2)}) collective-permute-start(bf16[64,2048]{1,0:T(8,128)(2,1)S(1)} %pack.7), channel_id=1, source_target_pairs={{0,2},{1,3},{2,0},{3,1},{4,6},{5,7},{6,4},{7,5},{8,10},{9,11},{10,... | collective-permute-start | bytes 786440 | tf_op jit(solution)/shard_map/ppermute | solution.py:33
  72.7 5.7 %collective-permute-start.15 = (bf16[64,2048]{1,0:T(8,128)(2,1)S(1)}, bf16[64,2048]{1,0:T(8,128)(2,1)S(1)}, u32[]{:S(2)}, u32[]{:S(2)}) collective-permute-start(bf16[64,2048]{1,0:T(8,128)(2,1)S(1)} %get-tuple-element.40), channel_id=1, source_target_pairs={{0,1},{1,0},{2,3},{3,2},{4,5},{5,4},{6,7},{7,6},{8,9},{9,8},{10,11... | collective-permute-start | bytes 786440 | tf_op jit(solution)/shard_map/ppermute | solution.py:33
  72.7 9.2 %collective-permute-start.16 = (bf16[64,2048]{1,0:T(8,128)(2,1)S(1)}, bf16[64,2048]{1,0:T(8,128)(2,1)S(1)}, u32[]{:S(2)}, u32[]{:S(2)}) collective-permute-start(bf16[64,2048]{1,0:T(8,128)(2,1)S(1)} %get-tuple-element.41), channel_id=1, source_target_pairs={{0,2},{1,3},{2,0},{3,1},{4,6},{5,7},{6,4},{7,5},{8,10},{9,11},{10,... | collective-permute-start | bytes 786440 | tf_op jit(solution)/shard_map/ppermute | solution.py:33
  74.2 12.3 %collective-permute-start.17 = (bf16[64,2048]{1,0:T(8,128)(2,1)S(1)}, bf16[64,2048]{1,0:T(8,128)(2,1)S(1)}, u32[]{:S(2)}, u32[]{:S(2)}) collective-permute-start(bf16[64,2048]{1,0:T(8,128)(2,1)S(1)} %get-tuple-element.42), channel_id=1, source_target_pairs={{0,3},{1,2},{2,1},{3,0},{4,7},{5,6},{6,5},{7,4},{8,11},{9,10},{10,... | collective-permute-start | bytes 786440 | tf_op jit(solution)/shard_map/ppermute | solution.py:33
  74.5 13.9 %collective-permute-start.12 = (bf16[64,2048]{1,0:T(8,128)(2,1)S(1)}, bf16[64,2048]{1,0:T(8,128)(2,1)S(1)}, u32[]{:S(2)}, u32[]{:S(2)}) collective-permute-start(bf16[64,2048]{1,0:T(8,128)(2,1)S(1)} %get-tuple-element.37), channel_id=1, source_target_pairs={{0,1},{1,0},{2,3},{3,2},{4,5},{5,4},{6,7},{7,6},{8,9},{9,8},{10,11... | collective-permute-start | bytes 786440 | tf_op jit(solution)/shard_map/ppermute | solution.py:33
  78.2 38.0 %collective-permute-start.18 = (bf16[64,3072]{1,0:T(8,128)(2,1)S(1)}, bf16[64,3072]{1,0:T(8,128)(2,1)S(1)}, u32[]{:S(2)}, u32[]{:S(2)}) collective-permute-start(bf16[64,3072]{1,0:T(8,128)(2,1)S(1)} %get-tuple-element.43), channel_id=1, source_target_pairs={{0,1},{1,0},{2,3},{3,2},{4,5},{5,4},{6,7},{7,6},{8,9},{9,8},{10,11... | collective-permute-start | bytes 1179656 | tf_op jit(solution)/shard_map/ppermute | solution.py:33
  78.4 14.7 %collective-permute-start.13 = (bf16[64,2048]{1,0:T(8,128)(2,1)S(1)}, bf16[64,2048]{1,0:T(8,128)(2,1)S(1)}, u32[]{:S(2)}, u32[]{:S(2)}) collective-permute-start(bf16[64,2048]{1,0:T(8,128)(2,1)S(1)} %get-tuple-element.38), channel_id=1, source_target_pairs={{0,2},{1,3},{2,0},{3,1},{4,6},{5,7},{6,4},{7,5},{8,10},{9,11},{10,... | collective-permute-start | bytes 786440 | tf_op jit(solution)/shard_map/ppermute | solution.py:33
  81.8 36.3 %collective-permute-start.19 = (bf16[64,3072]{1,0:T(8,128)(2,1)S(1)}, bf16[64,3072]{1,0:T(8,128)(2,1)S(1)}, u32[]{:S(2)}, u32[]{:S(2)}) collective-permute-start(bf16[64,3072]{1,0:T(8,128)(2,1)S(1)} %get-tuple-element.44), channel_id=1, source_target_pairs={{0,2},{1,3},{2,0},{3,1},{4,6},{5,7},{6,4},{7,5},{8,10},{9,11},{10,... | collective-permute-start | bytes 1179656 | tf_op jit(solution)/shard_map/ppermute | solution.py:33
  86.5 31.6 %collective-permute-start.20 = (bf16[64,3072]{1,0:T(8,128)(2,1)S(1)}, bf16[64,3072]{1,0:T(8,128)(2,1)S(1)}, u32[]{:S(2)}, u32[]{:S(2)}) collective-permute-start(bf16[64,3072]{1,0:T(8,128)(2,1)S(1)} %get-tuple-element.45), channel_id=1, source_target_pairs={{0,3},{1,2},{2,1},{3,0},{4,7},{5,6},{6,5},{7,4},{8,11},{9,10},{10,... | collective-permute-start | bytes 1179656 | tf_op jit(solution)/shard_map/ppermute | solution.py:33
  88.4 26.2 %collective-permute-start.14 = (bf16[64,2048]{1,0:T(8,128)(2,1)S(1)}, bf16[64,2048]{1,0:T(8,128)(2,1)S(1)}, u32[]{:S(2)}, u32[]{:S(2)}) collective-permute-start(bf16[64,2048]{1,0:T(8,128)(2,1)S(1)} %get-tuple-element.39), channel_id=1, source_target_pairs={{0,3},{1,2},{2,1},{3,0},{4,7},{5,6},{6,5},{7,4},{8,11},{9,10},{10,... | collective-permute-start | bytes 786440 | tf_op jit(solution)/shard_map/ppermute | solution.py:33
  93.1 26.1 %collective-permute-start.21 = (bf16[64,1024]{1,0:T(8,128)(2,1)S(1)}, bf16[64,1024]{1,0:T(8,128)(2,1)S(1)}, u32[]{:S(2)}, u32[]{:S(2)}) collective-permute-start(bf16[64,1024]{1,0:T(8,128)(2,1)S(1)} %get-tuple-element.46), channel_id=1, source_target_pairs={{0,1},{1,0},{2,3},{3,2},{4,5},{5,4},{6,7},{7,6},{8,9},{9,8},{10,11... | collective-permute-start | bytes 393224 | tf_op jit(solution)/shard_map/ppermute | solution.py:33
  114.6 6.4 %collective-permute-start.22 = (bf16[64,1024]{1,0:T(8,128)(2,1)S(1)}, bf16[64,1024]{1,0:T(8,128)(2,1)S(1)}, u32[]{:S(2)}, u32[]{:S(2)}) collective-permute-start(bf16[64,1024]{1,0:T(8,128)(2,1)S(1)} %get-tuple-element.47), channel_id=1, source_target_pairs={{0,2},{1,3},{2,0},{3,1},{4,6},{5,7},{6,4},{7,5},{8,10},{9,11},{10,... | collective-permute-start | bytes 393224 | tf_op jit(solution)/shard_map/ppermute | solution.py:33
  116.2 6.3 %collective-permute-start.23 = (bf16[64,1024]{1,0:T(8,128)(2,1)S(1)}, bf16[64,1024]{1,0:T(8,128)(2,1)S(1)}, u32[]{:S(2)}, u32[]{:S(2)}) collective-permute-start(bf16[64,1024]{1,0:T(8,128)(2,1)S(1)} %get-tuple-element.48), channel_id=1, source_target_pairs={{0,3},{1,2},{2,1},{3,0},{4,7},{5,6},{6,5},{7,4},{8,11},{9,10},{10,... | collective-permute-start | bytes 393224 | tf_op jit(solution)/shard_map/ppermute | solution.py:33

commit v2 on v1

--- a/solution.py
+++ b/solution.py
@@ -10,9 +10,9 @@
 HALO = 256
 ITERS = 6
 LANES = 128
-FIRST = [(0, 2), (2, 2), (4, 4)]
-OTHERS = [(0, 4), (4, 4)]
-STEPS = [(0, 2), (2, 2), (4, 3), (7, 1)]
+FIRST = [(0, 1), (1, 4), (5, 3)]
+OTHERS = [(0, 5), (5, 3)]
+STEPS = [(0, 1), (1, 4), (5, 2), (7, 1)]
 
 
 VMEM = pl.BlockSpec(memory_space=pltpu.VMEM)

time: 123 us -> 119 us (0.967)
  waiting for transfers between devices: 59 us -> 55.5 us
    ppermute x20, waiting for transfers between devices: 55.4 us -> 51.8 us  [swap(): return lax.ppermute(array, 'narrow', [(i, i ^ d) for i in range(n)])]
  transfers between devices with their start and end apart: 24 -> 24, of which waited for: 10 -> 10; matrix products, arithmetic and copies ran while one was open for 0% -> 0% of each run, Pallas kernels for 31% -> 32%
where the time goes in v2:
time: 119 us
  waiting for transfers between devices  55.5 us (47%)
  Pallas kernels  38.9 us (33%)
  starting transfers between devices  24.2 us (20%)
    ppermute x20, waiting for transfers between devices, swap(): return lax.ppermute(array, 'narrow', [(i, i ^ d) for i in range(n)])  51.8 us
    ppermute x20, starting transfers between devices, swap(): return lax.ppermute(array, 'narrow', [(i, i ^ d) for i in range(n)])  15.8 us
    pallas_call x4, Pallas kernels, apply(): pl.pallas_call(functools.partial(apply_kernel, parts), grid=(blocks,), in...  10.3 us
    pallas_call x1, Pallas kernels, transform(): pl.pallas_call(transform_kernel, grid=(1,), in_specs=[pl.BlockSpec((used,...  7.59 us
    pallas_call x1, Pallas kernels, gather(): pl.pallas_call(functools.partial(gather_kernel, regions), in_specs=[SMEM]...  6.91 us
    pallas_call x5, Pallas kernels, pack(): pl.pallas_call(functools.partial(pack_kernel, partners, cells, start), in...  5.42 us
    pallas_call x1, Pallas kernels, stats(): pl.pallas_call(stats_kernel, in_specs=[SMEM] + [VMEM] * (1 + len(parts)),...  4.46 us
    ppermute x2, starting transfers between devices, halo(): after = lax.ppermute(first, ('wide', 'narrow'), down)  4.26 us
  transfers between devices with their start and end apart: 24, of which 10 were waited for; matrix products, arithmetic and copies ran while one was open for 0% of the time, Pallas kernels for 32%

profile of v2, /device:TPU:0, one launch (start us, length us, event | category | flops | bytes accessed | tf_op | source)
XLA Modules:
  0.0 118.8 jit_solution(2022475566539829040)
XLA Ops:
  0.0 0.6 collective-permute-start.2
  0.6 1.2 %pack.5 = bf16[64,8192]{1,0:T(8,128)(2,1)S(1)} custom-call(bf16[64,32768]{1,0:T(8,128)(2,1)} %refs_0_.9), custom_call_target="tpu_custom_call" | custom-call | bytes 2097152 | tf_op jit(solution)/shard_map/pack/pallas_call | solution.py:64
  1.8 0.0 copy-start.3
  1.8 0.1 collective-permute-start.6
  2.0 2.6 %collective-permute-start.1 = (f32[72,256]{1,0:T(8,128)S(1)}, f32[72,256]{1,0:T(8,128)S(1)}, u32[]{:S(2)}, u32[]{:S(2)}) collective-permute-start(f32[72,256]{1,0:T(8,128)S(1)} %get-tuple-element.27), channel_id=1, source_target_pairs={{0,5},{1,4},{2,7},{3,6},{4,9},{5,8},{6,11},{7,10},{8,13},{9,12},{1... | collective-permute-start | bytes 221192 | tf_op jit(solution)/shard_map/ppermute | solution.py:40
  4.6 1.5 %collective-permute-start = (f32[72,256]{1,0:T(8,128)S(1)}, f32[72,256]{1,0:T(8,128)S(1)}, u32[]{:S(2)}, u32[]{:S(2)}) collective-permute-start(f32[72,256]{1,0:T(8,128)S(1)} %get-tuple-element.27), channel_id=1, source_target_pairs={{0,4},{1,5},{2,6},{3,7},{4,8},{5,9},{6,10},{7,11},{8,12},{9,13},{1... | collective-permute-start | bytes 221192 | tf_op jit(solution)/shard_map/ppermute | solution.py:40
  6.2 1.1 pack.8
  7.3 1.3 %collective-permute-start.10 = (bf16[64,5120]{1,0:T(8,128)(2,1)S(1)}, bf16[64,5120]{1,0:T(8,128)(2,1)S(1)}, u32[]{:S(2)}, u32[]{:S(2)}) collective-permute-start(bf16[64,5120]{1,0:T(8,128)(2,1)S(1)} %pack.8), channel_id=1, source_target_pairs={{0,3},{1,2},{2,1},{3,0},{4,7},{5,6},{6,5},{7,4},{8,11},{9,10},{10,... | collective-permute-start | bytes 1966088 | tf_op jit(solution)/shard_map/ppermute | solution.py:33
  8.6 1.2 %collective-permute-done.1.refs_1_ = f32[72,256]{1,0:T(8,128)S(1)} collective-permute-done((f32[72,256]{1,0:T(8,128)S(1)}, f32[72,256]{1,0:T(8,128)S(1)}, u32[]{:S(2)}, u32[]{:S(2)}) %collective-permute-start.1) | collective-permute-done | bytes 73760 | tf_op jit(solution)/shard_map/ppermute | solution.py:40
  9.9 2.4 %collective-permute-start.4 = (f32[72,256]{1,0:T(8,128)S(1)}, f32[72,256]{1,0:T(8,128)S(1)}, u32[]{:S(2)}, u32[]{:S(2)}) collective-permute-start(f32[72,256]{1,0:T(8,128)S(1)} %get-tuple-element.28), channel_id=1, source_target_pairs={{0,29},{1,28},{2,31},{3,30},{4,1},{5,0},{6,3},{7,2},{8,5},{9,4},{1... | collective-permute-start | bytes 221192 | tf_op jit(solution)/shard_map/ppermute | solution.py:41
  12.2 0.0 collective-permute-done.refs_0_.before_ref
  12.2 1.9 %collective-permute-start.3 = (f32[72,256]{1,0:T(8,128)S(1)}, f32[72,256]{1,0:T(8,128)S(1)}, u32[]{:S(2)}, u32[]{:S(2)}) collective-permute-start(f32[72,256]{1,0:T(8,128)S(1)} %get-tuple-element.28), channel_id=1, source_target_pairs={{0,28},{1,29},{2,30},{3,31},{4,0},{5,1},{6,2},{7,3},{8,4},{9,5},{1... | collective-permute-start | bytes 221192 | tf_op jit(solution)/shard_map/ppermute | solution.py:41
  14.1 0.5 collective-permute-done.4.refs_5_
  14.7 1.9 %collective-permute-done.3.refs_4_.after_ref = f32[72,256]{1,0:T(8,128)S(1)} collective-permute-done((f32[72,256]{1,0:T(8,128)S(1)}, f32[72,256]{1,0:T(8,128)S(1)}, u32[]{:S(2)}, u32[]{:S(2)}) %collective-permute-start.3) | collective-permute-done | bytes 73760 | tf_op jit(solution)/shard_map/ppermute | solution.py:41
  16.6 0.0 collective-permute-done.2.refs_3_
  16.6 6.9 %gather.1 = (bf16[1024,128]{1,0:T(8,128)(2,1)S(1)}, bf16[1024,128]{1,0:T(8,128)(2,1)S(1)}) custom-call(s32[4,1024]{1,0:T(4,128)S(1)} %copy-done.3, f32[72,256]{1,0:T(8,128)S(1)} %collective-permute-done.refs_0_.before_ref, f32[72,256]{1,0:T(8,128)S(1)} %collective-permute-done.1.refs_1_, bf16[64,4096]{1,0:T(8,128)(2,1)S(1)} %copy-done, ...), custom_call_target="tpu_custom_call" | custom-call | bytes 6815744 | tf_op jit(solution)/shard_map/gather/pallas_call | solution.py:141
  23.5 1.6 %collective-permute-start.5 = (bf16[1024,128]{1,0:T(8,128)(2,1)S(1)}, bf16[1024,128]{1,0:T(8,128)(2,1)S(1)}, u32[]{:S(2)}, u32[]{:S(2)}) collective-permute-start(bf16[1024,128]{1,0:T(8,128)(2,1)S(1)} %get-tuple-element.30), channel_id=1, source_target_pairs={{0,2},{1,3},{2,0},{3,1},{4,6},{5,7},{6,4},{7,5},{8,10},{9,11},{10,... | collective-permute-start | bytes 786440 | tf_op jit(solution)/shard_map/ppermute | solution.py:33
  25.2 1.0 pack.7
  26.2 0.0 copy-start.4
  26.2 0.5 collective-permute-start.9
  26.7 0.9 pack.9
  27.7 1.6 %collective-permute-start.11 = (bf16[64,1024]{1,0:T(8,128)(2,1)S(1)}, bf16[64,1024]{1,0:T(8,128)(2,1)S(1)}, u32[]{:S(2)}, u32[]{:S(2)}) collective-permute-start(bf16[64,1024]{1,0:T(8,128)(2,1)S(1)} %pack.9), channel_id=1, source_target_pairs={{0,2},{1,3},{2,0},{3,1},{4,6},{5,7},{6,4},{7,5},{8,10},{9,11},{10,... | collective-permute-start | bytes 393224 | tf_op jit(solution)/shard_map/ppermute | solution.py:33
  29.3 1.1 pack.6
  30.4 14.7 %collective-permute-done.11.refs_2_ = bf16[64,1024]{1,0:T(8,128)(2,1)S(1)} collective-permute-done((bf16[64,1024]{1,0:T(8,128)(2,1)S(1)}, bf16[64,1024]{1,0:T(8,128)(2,1)S(1)}, u32[]{:S(2)}, u32[]{:S(2)}) %collective-permute-start.11) | collective-permute-done | bytes 131104 | tf_op jit(solution)/shard_map/ppermute | solution.py:33
  45.2 1.5 %collective-permute-start.7 = (bf16[64,3072]{1,0:T(8,128)(2,1)S(1)}, bf16[64,3072]{1,0:T(8,128)(2,1)S(1)}, u32[]{:S(2)}, u32[]{:S(2)}) collective-permute-start(bf16[64,3072]{1,0:T(8,128)(2,1)S(1)} %get-tuple-element.31), channel_id=1, source_target_pairs={{0,2},{1,3},{2,0},{3,1},{4,6},{5,7},{6,4},{7,5},{8,10},{9,11},{10,... | collective-permute-start | bytes 1179656 | tf_op jit(solution)/shard_map/ppermute | solution.py:33
  46.7 4.5 %stats.1.stats_ref = f32[1024,8]{1,0:T(8,128)S(1)} custom-call(s32[4,1024]{1,0:T(4,128)S(1)} %copy-done.3, f32[1,1024]{1,0:T(1,128)S(1)} %copy-done.4, f32[72,256]{1,0:T(8,128)S(1)} %collective-permute-done.refs_0_.before_ref, f32[1,4096]{1,0:T(1,128)S(1)} %bitcast.4, f32[1,4096]{1,0:T(1,128)S(1)} %bitcast.7, ...), custom_call_target="tpu_custom_call" | custom-call | bytes 2883584 | tf_op jit(solution)/shard_map/stats/pallas_call | solution.py:189
  51.2 0.0 collective-permute-done.5.refs_0_
  51.2 0.1 collective-permute-start.8
  51.2 7.6 %transform.1.weights_ref = bf16[256,256]{1,0:T(8,128)(2,1)S(1)} custom-call(bf16[1024,128]{1,0:T(8,128)(2,1)S(1)} %get-tuple-element.29.own_ref, f32[1024,8]{1,0:T(8,128)S(1)} %stats.1.stats_ref, bf16[1024,128]{1,0:T(8,128)(2,1)S(1)} %collective-permute-done.5.refs_0_), custom_call_target="tpu_custom_call" | custom-call | flops 3221225472 | bytes 1048576 | tf_op jit(solution)/shard_map/transform/pallas_call | solution.py:239
  58.8 0.0 collective-permute-done.10.refs_3_
  58.9 0.0 collective-permute-done.6.refs_1_
  58.9 1.9 %apply.4 = (bf16[64,32768]{1,0:T(8,128)(2,1)}, bf16[64,1024]{1,0:T(8,128)(2,1)S(1)}, bf16[64,1024]{1,0:T(8,128)(2,1)S(1)}, bf16[64,1024]{1,0:T(8,128)(2,1)S(1)}) custom-call(bf16[256,256]{1,0:T(8,128)(2,1)S(1)} %transform.1.weights_ref, bf16[64,32768]{1,0:T(8,128)(2,1)} %refs_0_.9, bf16[64,8192]{1,0:T(8,128)(2,1)S(1)} %collective-permute-done.6.refs_1_, ...), custom_call_target="tpu_custom_call" | custom-call | flops 134217728 | bytes 1048576 | tf_op jit(solution)/shard_map/apply/pallas_call | solution.py:281
  60.8 0.6 collective-permute-start.12
  61.4 0.0 collective-permute-done.9.refs_2_
  61.4 3.9 %apply.5 = (bf16[64,32768]{1,0:T(8,128)(2,1)}, bf16[64,4096]{1,0:T(8,128)(2,1)S(1)}, bf16[64,4096]{1,0:T(8,128)(2,1)S(1)}, bf16[64,4096]{1,0:T(8,128)(2,1)S(1)}) custom-call(bf16[256,256]{1,0:T(8,128)(2,1)S(1)} %transform.1.weights_ref, bf16[64,32768]{1,0:T(8,128)(2,1)} %refs_0_.9, ...), custom_call_target="tpu_custom_call", output_to_operand_aliasing={{0}: (5, {})} | custom-call | flops 536870912 | bytes 4194304 | tf_op jit(solution)/shard_map/apply/pallas_call | solution.py:281
  65.4 0.0 collective-permute-start.15
  65.4 1.5 %collective-permute-start.16 = (bf16[64,4096]{1,0:T(8,128)(2,1)S(1)}, bf16[64,4096]{1,0:T(8,128)(2,1)S(1)}, u32[]{:S(2)}, u32[]{:S(2)}) collective-permute-start(bf16[64,4096]{1,0:T(8,128)(2,1)S(1)} %get-tuple-element.41), channel_id=1, source_target_pairs={{0,2},{1,3},{2,0},{3,1},{4,6},{5,7},{6,4},{7,5},{8,10},{9,11},{10,... | collective-permute-start | bytes 1572872 | tf_op jit(solution)/shard_map/ppermute | solution.py:33
  66.9 0.0 collective-permute-done.7.refs_2_
  66.9 0.3 collective-permute-start.17
  67.2 1.5 %collective-permute-start.13 = (bf16[64,1024]{1,0:T(8,128)(2,1)S(1)}, bf16[64,1024]{1,0:T(8,128)(2,1)S(1)}, u32[]{:S(2)}, u32[]{:S(2)}) collective-permute-start(bf16[64,1024]{1,0:T(8,128)(2,1)S(1)} %get-tuple-element.38), channel_id=1, source_target_pairs={{0,2},{1,3},{2,0},{3,1},{4,6},{5,7},{6,4},{7,5},{8,10},{9,11},{10,... | collective-permute-start | bytes 393224 | tf_op jit(solution)/shard_map/ppermute | solution.py:33
  68.7 2.5 %apply.6 = (bf16[64,32768]{1,0:T(8,128)(2,1)}, bf16[64,2048]{1,0:T(8,128)(2,1)S(1)}, bf16[64,2048]{1,0:T(8,128)(2,1)S(1)}, bf16[64,2048]{1,0:T(8,128)(2,1)S(1)}) custom-call(bf16[256,256]{1,0:T(8,128)(2,1)S(1)} %transform.1.weights_ref, bf16[64,32768]{1,0:T(8,128)(2,1)} %refs_0_.9, ...), custom_call_target="tpu_custom_call", output_to_operand_aliasing={{0}: (5, {})} | custom-call | flops 268435456 | bytes 2097152 | tf_op jit(solution)/shard_map/apply/pallas_call | solution.py:281
  71.2 0.0 collective-permute-done.12.refs_0_
  71.2 0.0 collective-permute-start.18
  71.2 22.5 %collective-permute-done.13.refs_1_ = bf16[64,1024]{1,0:T(8,128)(2,1)S(1)} collective-permute-done((bf16[64,1024]{1,0:T(8,128)(2,1)S(1)}, bf16[64,1024]{1,0:T(8,128)(2,1)S(1)}, u32[]{:S(2)}, u32[]{:S(2)}) %collective-permute-start.13) | collective-permute-done | bytes 131104 | tf_op jit(solution)/shard_map/ppermute | solution.py:33
  93.7 0.7 collective-permute-start.14
  94.5 5.0 %collective-permute-done.14.refs_2_ = bf16[64,1024]{1,0:T(8,128)(2,1)S(1)} collective-permute-done((bf16[64,1024]{1,0:T(8,128)(2,1)S(1)}, bf16[64,1024]{1,0:T(8,128)(2,1)S(1)}, u32[]{:S(2)}, u32[]{:S(2)}) %collective-permute-start.14) | collective-permute-done | bytes 131104 | tf_op jit(solution)/shard_map/ppermute | solution.py:33
  99.5 1.4 %collective-permute-start.19 = (bf16[64,2048]{1,0:T(8,128)(2,1)S(1)}, bf16[64,2048]{1,0:T(8,128)(2,1)S(1)}, u32[]{:S(2)}, u32[]{:S(2)}) collective-permute-start(bf16[64,2048]{1,0:T(8,128)(2,1)S(1)} %get-tuple-element.44), channel_id=1, source_target_pairs={{0,2},{1,3},{2,0},{3,1},{4,6},{5,7},{6,4},{7,5},{8,10},{9,11},{10,... | collective-permute-start | bytes 786440 | tf_op jit(solution)/shard_map/ppermute | solution.py:33
  100.9 0.1 collective-permute-start.20
  100.9 1.9 %apply.7 = (bf16[64,32768]{1,0:T(8,128)(2,1)}, bf16[64,1024]{1,0:T(8,128)(2,1)S(1)}, bf16[64,1024]{1,0:T(8,128)(2,1)S(1)}, bf16[64,1024]{1,0:T(8,128)(2,1)S(1)}) custom-call(bf16[256,256]{1,0:T(8,128)(2,1)S(1)} %transform.1.weights_ref, bf16[64,32768]{1,0:T(8,128)(2,1)} %refs_0_.9, ...), custom_call_target="tpu_custom_call", output_to_operand_aliasing={{0}: (5, {})} | custom-call | flops 134217728 | bytes 1048576 | tf_op jit(solution)/shard_map/apply/pallas_call | solution.py:281
  102.9 0.0 collective-permute-done.15.refs_0_
  102.9 0.7 collective-permute-start.21
  103.6 1.4 %collective-permute-start.22 = (bf16[64,1024]{1,0:T(8,128)(2,1)S(1)}, bf16[64,1024]{1,0:T(8,128)(2,1)S(1)}, u32[]{:S(2)}, u32[]{:S(2)}) collective-permute-start(bf16[64,1024]{1,0:T(8,128)(2,1)S(1)} %get-tuple-element.47), channel_id=1, source_target_pairs={{0,2},{1,3},{2,0},{3,1},{4,6},{5,7},{6,4},{7,5},{8,10},{9,11},{10,... | collective-permute-start | bytes 393224 | tf_op jit(solution)/shard_map/ppermute | solution.py:33
  105.0 0.0 collective-permute-done.17.refs_2_
  105.0 0.0 collective-permute-start.23
  105.0 0.8 place.5.result_ref
  105.8 1.2 place.6.result_ref
  106.9 1.7 %collective-permute-done.19.refs_1_ = bf16[64,2048]{1,0:T(8,128)(2,1)S(1)} collective-permute-done((bf16[64,2048]{1,0:T(8,128)(2,1)S(1)}, bf16[64,2048]{1,0:T(8,128)(2,1)S(1)}, u32[]{:S(2)}, u32[]{:S(2)}) %collective-permute-start.19) | collective-permute-done | bytes 262176 | tf_op jit(solution)/shard_map/ppermute | solution.py:33
  108.6 4.5 %collective-permute-done.20.refs_2_ = bf16[64,2048]{1,0:T(8,128)(2,1)S(1)} collective-permute-done((bf16[64,2048]{1,0:T(8,128)(2,1)S(1)}, bf16[64,2048]{1,0:T(8,128)(2,1)S(1)}, u32[]{:S(2)}, u32[]{:S(2)}) %collective-permute-start.20) | collective-permute-done | bytes 262176 | tf_op jit(solution)/shard_map/ppermute | solution.py:33
  113.2 0.9 place.7.result_ref
  114.1 0.0 collective-permute-done.21.refs_0_
  114.1 3.0 %collective-permute-done.22.refs_1_ = bf16[64,1024]{1,0:T(8,128)(2,1)S(1)} collective-permute-done((bf16[64,1024]{1,0:T(8,128)(2,1)S(1)}, bf16[64,1024]{1,0:T(8,128)(2,1)S(1)}, u32[]{:S(2)}, u32[]{:S(2)}) %collective-permute-start.22) | collective-permute-done | bytes 131104 | tf_op jit(solution)/shard_map/ppermute | solution.py:33
  117.1 0.7 place.8.result_ref
  117.8 0.4 collective-permute-done.23.refs_0_
  118.2 0.7 place.9
  (12 shorter events, 0.0 us)
Async XLA Ops:
  0.0 2.0 %copy-start = (bf16[64,4096]{1,0:T(8,128)(2,1)S(1)}, bf16[64,4096]{1,0:T(8,128)(2,1)}, u32[]{:S(2)}) copy-start(bf16[64,4096]{1,0:T(8,128)(2,1)} %refs_2_.1) | copy-start | bytes 1572868
  0.0 2.0 %copy-start.2 = (f32[4096]{0:T(1024)S(1)}, f32[4096]{0:T(1024)}, u32[]{:S(2)}) copy-start(f32[4096]{0:T(1024)} %param.9) | copy-start | bytes 49156
  0.0 2.0 %copy-start.1 = (f32[4096]{0:T(1024)S(1)}, f32[4096]{0:T(1024)}, u32[]{:S(2)}) copy-start(f32[4096]{0:T(1024)} %param.8) | copy-start | bytes 49156
  0.0 16.6 %collective-permute-start.2 = (bf16[64,4096]{1,0:T(8,128)(2,1)}, bf16[64,4096]{1,0:T(8,128)(2,1)S(1)}, u32[]{:S(2)}, u32[]{:S(2)}) collective-permute-start(bf16[64,4096]{1,0:T(8,128)(2,1)} %refs_2_.1), channel_id=1, source_target_pairs={{0,1},{1,0},{2,3},{3,2},{4,5},{5,4},{6,7},{7,6},{8,9},{9,8},{10,11... | collective-permute-start | bytes 1572872 | tf_op jit(solution)/shard_map/ppermute | solution.py:33
  1.8 14.8 %copy-start.3 = (s32[4,1024]{1,0:T(4,128)S(1)}, s32[4,1024]{1,0:T(4,128)}, u32[]{:S(2)}) copy-start(s32[4,1024]{1,0:T(4,128)} %pick_ref.3) | copy-start | bytes 49156
  1.8 57.0 %collective-permute-start.6 = (bf16[64,8192]{1,0:T(8,128)(2,1)S(1)}, bf16[64,8192]{1,0:T(8,128)(2,1)S(1)}, u32[]{:S(2)}, u32[]{:S(2)}) collective-permute-start(bf16[64,8192]{1,0:T(8,128)(2,1)S(1)} %pack.5), channel_id=1, source_target_pairs={{0,1},{1,0},{2,3},{3,2},{4,5},{5,4},{6,7},{7,6},{8,9},{9,8},{10,11... | collective-permute-start | bytes 3145736 | tf_op jit(solution)/shard_map/ppermute | solution.py:33
  2.0 7.9 %collective-permute-start.1 = (f32[72,256]{1,0:T(8,128)S(1)}, f32[72,256]{1,0:T(8,128)S(1)}, u32[]{:S(2)}, u32[]{:S(2)}) collective-permute-start(f32[72,256]{1,0:T(8,128)S(1)} %get-tuple-element.27), channel_id=1, source_target_pairs={{0,5},{1,4},{2,7},{3,6},{4,9},{5,8},{6,11},{7,10},{8,13},{9,12},{1... | collective-permute-start | bytes 221192 | tf_op jit(solution)/shard_map/ppermute | solution.py:40
  4.6 7.6 %collective-permute-start = (f32[72,256]{1,0:T(8,128)S(1)}, f32[72,256]{1,0:T(8,128)S(1)}, u32[]{:S(2)}, u32[]{:S(2)}) collective-permute-start(f32[72,256]{1,0:T(8,128)S(1)} %get-tuple-element.27), channel_id=1, source_target_pairs={{0,4},{1,5},{2,6},{3,7},{4,8},{5,9},{6,10},{7,11},{8,12},{9,13},{1... | collective-permute-start | bytes 221192 | tf_op jit(solution)/shard_map/ppermute | solution.py:40
  7.3 51.6 %collective-permute-start.10 = (bf16[64,5120]{1,0:T(8,128)(2,1)S(1)}, bf16[64,5120]{1,0:T(8,128)(2,1)S(1)}, u32[]{:S(2)}, u32[]{:S(2)}) collective-permute-start(bf16[64,5120]{1,0:T(8,128)(2,1)S(1)} %pack.8), channel_id=1, source_target_pairs={{0,3},{1,2},{2,1},{3,0},{4,7},{5,6},{6,5},{7,4},{8,11},{9,10},{10,... | collective-permute-start | bytes 1966088 | tf_op jit(solution)/shard_map/ppermute | solution.py:33
  9.9 4.8 %collective-permute-start.4 = (f32[72,256]{1,0:T(8,128)S(1)}, f32[72,256]{1,0:T(8,128)S(1)}, u32[]{:S(2)}, u32[]{:S(2)}) collective-permute-start(f32[72,256]{1,0:T(8,128)S(1)} %get-tuple-element.28), channel_id=1, source_target_pairs={{0,29},{1,28},{2,31},{3,30},{4,1},{5,0},{6,3},{7,2},{8,5},{9,4},{1... | collective-permute-start | bytes 221192 | tf_op jit(solution)/shard_map/ppermute | solution.py:41
  12.2 4.4 %collective-permute-start.3 = (f32[72,256]{1,0:T(8,128)S(1)}, f32[72,256]{1,0:T(8,128)S(1)}, u32[]{:S(2)}, u32[]{:S(2)}) collective-permute-start(f32[72,256]{1,0:T(8,128)S(1)} %get-tuple-element.28), channel_id=1, source_target_pairs={{0,28},{1,29},{2,30},{3,31},{4,0},{5,1},{6,2},{7,3},{8,4},{9,5},{1... | collective-permute-start | bytes 221192 | tf_op jit(solution)/shard_map/ppermute | solution.py:41
  23.5 27.6 %collective-permute-start.5 = (bf16[1024,128]{1,0:T(8,128)(2,1)S(1)}, bf16[1024,128]{1,0:T(8,128)(2,1)S(1)}, u32[]{:S(2)}, u32[]{:S(2)}) collective-permute-start(bf16[1024,128]{1,0:T(8,128)(2,1)S(1)} %get-tuple-element.30), channel_id=1, source_target_pairs={{0,2},{1,3},{2,0},{3,1},{4,6},{5,7},{6,4},{7,5},{8,10},{9,11},{10,... | collective-permute-start | bytes 786440 | tf_op jit(solution)/shard_map/ppermute | solution.py:33
  26.2 20.5 %copy-start.4 = (f32[1,1024]{1,0:T(1,128)S(1)}, f32[1,1024]{1,0:T(1,128)}, u32[]{:S(2)}) copy-start(f32[1,1024]{1,0:T(1,128)} %taper_ref.1) | copy-start | bytes 12292
  26.2 35.2 %collective-permute-start.9 = (bf16[64,4096]{1,0:T(8,128)(2,1)S(1)}, bf16[64,4096]{1,0:T(8,128)(2,1)S(1)}, u32[]{:S(2)}, u32[]{:S(2)}) collective-permute-start(bf16[64,4096]{1,0:T(8,128)(2,1)S(1)} %pack.7), channel_id=1, source_target_pairs={{0,2},{1,3},{2,0},{3,1},{4,6},{5,7},{6,4},{7,5},{8,10},{9,11},{10,... | collective-permute-start | bytes 1572872 | tf_op jit(solution)/shard_map/ppermute | solution.py:33
  27.7 17.5 %collective-permute-start.11 = (bf16[64,1024]{1,0:T(8,128)(2,1)S(1)}, bf16[64,1024]{1,0:T(8,128)(2,1)S(1)}, u32[]{:S(2)}, u32[]{:S(2)}) collective-permute-start(bf16[64,1024]{1,0:T(8,128)(2,1)S(1)} %pack.9), channel_id=1, source_target_pairs={{0,2},{1,3},{2,0},{3,1},{4,6},{5,7},{6,4},{7,5},{8,10},{9,11},{10,... | collective-permute-start | bytes 393224 | tf_op jit(solution)/shard_map/ppermute | solution.py:33
  45.2 21.7 %collective-permute-start.7 = (bf16[64,3072]{1,0:T(8,128)(2,1)S(1)}, bf16[64,3072]{1,0:T(8,128)(2,1)S(1)}, u32[]{:S(2)}, u32[]{:S(2)}) collective-permute-start(bf16[64,3072]{1,0:T(8,128)(2,1)S(1)} %get-tuple-element.31), channel_id=1, source_target_pairs={{0,2},{1,3},{2,0},{3,1},{4,6},{5,7},{6,4},{7,5},{8,10},{9,11},{10,... | collective-permute-start | bytes 1179656 | tf_op jit(solution)/shard_map/ppermute | solution.py:33
  51.2 16.1 %collective-permute-start.8 = (bf16[64,3072]{1,0:T(8,128)(2,1)S(1)}, bf16[64,3072]{1,0:T(8,128)(2,1)S(1)}, u32[]{:S(2)}, u32[]{:S(2)}) collective-permute-start(bf16[64,3072]{1,0:T(8,128)(2,1)S(1)} %get-tuple-element.32), channel_id=1, source_target_pairs={{0,3},{1,2},{2,1},{3,0},{4,7},{5,6},{6,5},{7,4},{8,11},{9,10},{10,... | collective-permute-start | bytes 1179656 | tf_op jit(solution)/shard_map/ppermute | solution.py:33
  60.8 10.4 %collective-permute-start.12 = (bf16[64,1024]{1,0:T(8,128)(2,1)S(1)}, bf16[64,1024]{1,0:T(8,128)(2,1)S(1)}, u32[]{:S(2)}, u32[]{:S(2)}) collective-permute-start(bf16[64,1024]{1,0:T(8,128)(2,1)S(1)} %get-tuple-element.37), channel_id=1, source_target_pairs={{0,1},{1,0},{2,3},{3,2},{4,5},{5,4},{6,7},{7,6},{8,9},{9,8},{10,11... | collective-permute-start | bytes 393224 | tf_op jit(solution)/shard_map/ppermute | solution.py:33
  65.4 37.5 %collective-permute-start.15 = (bf16[64,4096]{1,0:T(8,128)(2,1)S(1)}, bf16[64,4096]{1,0:T(8,128)(2,1)S(1)}, u32[]{:S(2)}, u32[]{:S(2)}) collective-permute-start(bf16[64,4096]{1,0:T(8,128)(2,1)S(1)} %get-tuple-element.40), channel_id=1, source_target_pairs={{0,1},{1,0},{2,3},{3,2},{4,5},{5,4},{6,7},{7,6},{8,9},{9,8},{10,11... | collective-permute-start | bytes 1572872 | tf_op jit(solution)/shard_map/ppermute | solution.py:33
  65.4 38.2 %collective-permute-start.16 = (bf16[64,4096]{1,0:T(8,128)(2,1)S(1)}, bf16[64,4096]{1,0:T(8,128)(2,1)S(1)}, u32[]{:S(2)}, u32[]{:S(2)}) collective-permute-start(bf16[64,4096]{1,0:T(8,128)(2,1)S(1)} %get-tuple-element.41), channel_id=1, source_target_pairs={{0,2},{1,3},{2,0},{3,1},{4,6},{5,7},{6,4},{7,5},{8,10},{9,11},{10,... | collective-permute-start | bytes 1572872 | tf_op jit(solution)/shard_map/ppermute | solution.py:33
  66.9 38.0 %collective-permute-start.17 = (bf16[64,4096]{1,0:T(8,128)(2,1)S(1)}, bf16[64,4096]{1,0:T(8,128)(2,1)S(1)}, u32[]{:S(2)}, u32[]{:S(2)}) collective-permute-start(bf16[64,4096]{1,0:T(8,128)(2,1)S(1)} %get-tuple-element.42), channel_id=1, source_target_pairs={{0,3},{1,2},{2,1},{3,0},{4,7},{5,6},{6,5},{7,4},{8,11},{9,10},{10,... | collective-permute-start | bytes 1572872 | tf_op jit(solution)/shard_map/ppermute | solution.py:33
  67.2 26.5 %collective-permute-start.13 = (bf16[64,1024]{1,0:T(8,128)(2,1)S(1)}, bf16[64,1024]{1,0:T(8,128)(2,1)S(1)}, u32[]{:S(2)}, u32[]{:S(2)}) collective-permute-start(bf16[64,1024]{1,0:T(8,128)(2,1)S(1)} %get-tuple-element.38), channel_id=1, source_target_pairs={{0,2},{1,3},{2,0},{3,1},{4,6},{5,7},{6,4},{7,5},{8,10},{9,11},{10,... | collective-permute-start | bytes 393224 | tf_op jit(solution)/shard_map/ppermute | solution.py:33
  71.2 29.7 %collective-permute-start.18 = (bf16[64,2048]{1,0:T(8,128)(2,1)S(1)}, bf16[64,2048]{1,0:T(8,128)(2,1)S(1)}, u32[]{:S(2)}, u32[]{:S(2)}) collective-permute-start(bf16[64,2048]{1,0:T(8,128)(2,1)S(1)} %get-tuple-element.43), channel_id=1, source_target_pairs={{0,1},{1,0},{2,3},{3,2},{4,5},{5,4},{6,7},{7,6},{8,9},{9,8},{10,11... | collective-permute-start | bytes 786440 | tf_op jit(solution)/shard_map/ppermute | solution.py:33
  93.7 5.7 %collective-permute-start.14 = (bf16[64,1024]{1,0:T(8,128)(2,1)S(1)}, bf16[64,1024]{1,0:T(8,128)(2,1)S(1)}, u32[]{:S(2)}, u32[]{:S(2)}) collective-permute-start(bf16[64,1024]{1,0:T(8,128)(2,1)S(1)} %get-tuple-element.39), channel_id=1, source_target_pairs={{0,3},{1,2},{2,1},{3,0},{4,7},{5,6},{6,5},{7,4},{8,11},{9,10},{10,... | collective-permute-start | bytes 393224 | tf_op jit(solution)/shard_map/ppermute | solution.py:33
  99.5 9.2 %collective-permute-start.19 = (bf16[64,2048]{1,0:T(8,128)(2,1)S(1)}, bf16[64,2048]{1,0:T(8,128)(2,1)S(1)}, u32[]{:S(2)}, u32[]{:S(2)}) collective-permute-start(bf16[64,2048]{1,0:T(8,128)(2,1)S(1)} %get-tuple-element.44), channel_id=1, source_target_pairs={{0,2},{1,3},{2,0},{3,1},{4,6},{5,7},{6,4},{7,5},{8,10},{9,11},{10,... | collective-permute-start | bytes 786440 | tf_op jit(solution)/shard_map/ppermute | solution.py:33
  100.9 12.3 %collective-permute-start.20 = (bf16[64,2048]{1,0:T(8,128)(2,1)S(1)}, bf16[64,2048]{1,0:T(8,128)(2,1)S(1)}, u32[]{:S(2)}, u32[]{:S(2)}) collective-permute-start(bf16[64,2048]{1,0:T(8,128)(2,1)S(1)} %get-tuple-element.45), channel_id=1, source_target_pairs={{0,3},{1,2},{2,1},{3,0},{4,7},{5,6},{6,5},{7,4},{8,11},{9,10},{10,... | collective-permute-start | bytes 786440 | tf_op jit(solution)/shard_map/ppermute | solution.py:33
  102.9 11.2 %collective-permute-start.21 = (bf16[64,1024]{1,0:T(8,128)(2,1)S(1)}, bf16[64,1024]{1,0:T(8,128)(2,1)S(1)}, u32[]{:S(2)}, u32[]{:S(2)}) collective-permute-start(bf16[64,1024]{1,0:T(8,128)(2,1)S(1)} %get-tuple-element.46), channel_id=1, source_target_pairs={{0,1},{1,0},{2,3},{3,2},{4,5},{5,4},{6,7},{7,6},{8,9},{9,8},{10,11... | collective-permute-start | bytes 393224 | tf_op jit(solution)/shard_map/ppermute | solution.py:33
  103.6 13.5 %collective-permute-start.22 = (bf16[64,1024]{1,0:T(8,128)(2,1)S(1)}, bf16[64,1024]{1,0:T(8,128)(2,1)S(1)}, u32[]{:S(2)}, u32[]{:S(2)}) collective-permute-start(bf16[64,1024]{1,0:T(8,128)(2,1)S(1)} %get-tuple-element.47), channel_id=1, source_target_pairs={{0,2},{1,3},{2,0},{3,1},{4,6},{5,7},{6,4},{7,5},{8,10},{9,11},{10,... | collective-permute-start | bytes 393224 | tf_op jit(solution)/shard_map/ppermute | solution.py:33
  105.0 13.2 %collective-permute-start.23 = (bf16[64,1024]{1,0:T(8,128)(2,1)S(1)}, bf16[64,1024]{1,0:T(8,128)(2,1)S(1)}, u32[]{:S(2)}, u32[]{:S(2)}) collective-permute-start(bf16[64,1024]{1,0:T(8,128)(2,1)S(1)} %get-tuple-element.48), channel_id=1, source_target_pairs={{0,3},{1,2},{2,1},{3,0},{4,7},{5,6},{6,5},{7,4},{8,11},{9,10},{10,... | collective-permute-start | bytes 393224 | tf_op jit(solution)/shard_map/ppermute | solution.py:33
